TPU v7x, 512 devices: a whole 4x4x16 slice. The times are simulated.
512 devices in a mesh: dp: 8 (over x_hi, y), fsdp: 16 (over z), tensor: 4 (over x_lo, core).
Axes of the slice: x: 4 (x_hi: 2, x_lo: 2; x = x_hi * 2 + x_lo), y: 4, z: 16, core: 2. Of those that a mesh axis runs over, the one named last changes fastest.
Arguments:
- grad_part: bfloat16 [8, 16, 2048, 1024], P('dp', 'fsdp', None, 'tensor'), may hold values from -900 to 900
- gain_grad_part: bfloat16 [8, 16, 4, 2048], P('dp', 'fsdp', 'tensor'), may hold values from -840 to 840
- master: float32 [2048, 1024], P('fsdp', 'tensor'), may hold values from -0.005 to 0.005
- moment_one: float32 [2048, 1024], P('fsdp', 'tensor'), may hold values from -2.4 to 2.4
- moment_two: float32 [2048, 1024], P('fsdp', 'tensor'), may hold values from 0.05 to 1.5
- teacher: float32 [2048, 1024], P('fsdp', 'tensor'), may hold values from -0.005 to 0.005
- gain_master: float32 [2048], P('fsdp'), may hold values from -0.008 to 0.008
- gain_moment_one: float32 [2048], P('fsdp'), may hold values from -18 to 18
- gain_moment_two: float32 [2048], P('fsdp'), may hold values from 2 to 32
- gain_teacher: float32 [2048], P('fsdp'), may hold values from -0.008 to 0.008
Outputs:
- weights: bfloat16 [2048, 1024], P(None, 'tensor')
- gain_weights: bfloat16 [2048], replicated
- master_new: float32 [2048, 1024], P('fsdp', 'tensor')
- moment_one_new: float32 [2048, 1024], P('fsdp', 'tensor')
- moment_two_new: float32 [2048, 1024], P('fsdp', 'tensor')
- teacher_new: float32 [2048, 1024], P('fsdp', 'tensor')
- gain_master_new: float32 [2048], P('fsdp')
- gain_moment_one_new: float32 [2048], P('fsdp')
- gain_moment_two_new: float32 [2048], P('fsdp')
- gain_teacher_new: float32 [2048], P('fsdp')
All inputs are finite; a program needn't handle non-finite values.
Results may differ from a plain program's by a relative error of at most 0.001.
Values may be sent and summed in bfloat16 or wider, within the bound.
No kernel may reach another device: no remote copies, remote signals or barrier semaphores. Data moves between devices by JAX's collectives and lax.ppermute only.
A program may use at most 64 MiB of HBM per device.

v0:
```python
import math

import jax
import jax.numpy as jnp
from jax import lax
from jax.sharding import PartitionSpec as P

D = 2048
HEADS = 8
HEAD = 128
STEP = 20


beta_one = 0.9
beta_two = 0.95
learn_rate = 0.001
teacher_keep = 0.996
clip_level = 2.0
tiny_epsilon = 1e-08


def adamw(parameter, first_moment, second_moment, gradient, clip_factor, weight_decay, shadow):
    scaled = gradient * clip_factor
    first_new = beta_one * first_moment + (1.0 - beta_one) * scaled
    second_new = beta_two * second_moment + (1.0 - beta_two) * scaled * scaled
    corr_one = 1.0 - beta_one**STEP
    corr_two = 1.0 - beta_two**STEP
    direction = first_new / corr_one / (jnp.sqrt(second_new / corr_two) + tiny_epsilon)
    parameter_new = parameter - learn_rate * (direction + weight_decay * parameter)
    shadow_new = teacher_keep * shadow + (1.0 - teacher_keep) * parameter_new
    return (parameter_new, first_new, second_new, shadow_new)


def shards(
    grad_part,
    gain_grad_part,
    master,
    moment_one,
    moment_two,
    teacher,
    gain_master,
    gain_moment_one,
    gain_moment_two,
    gain_teacher,
):
    tensor_count = lax.axis_size("tensor")
    local_gain = gain_grad_part[0, 0, 0].astype(jnp.float32)
    local_gain = lax.psum(local_gain, "tensor")
    local_grad = grad_part[0, 0].astype(jnp.float32)
    owned_rows, owned_gain = (
        lax.psum_scatter(local_grad, "fsdp", scatter_dimension=0, tiled=True),
        lax.psum_scatter(local_gain, "fsdp", scatter_dimension=0, tiled=True),
    )
    owned_rows, owned_gain = lax.psum((owned_rows, owned_gain), "dp")
    own_squares = jnp.sum(owned_rows * owned_rows) + jnp.sum(owned_gain * owned_gain) / tensor_count
    total_squares = lax.psum(own_squares, ("fsdp", "tensor"))
    clip_limit = clip_level * math.sqrt(D * HEADS * HEAD + D)
    clip_factor = clip_limit / (jnp.sqrt(total_squares) + 1e-06)
    matrix_state = adamw(master, moment_one, moment_two, owned_rows, clip_factor, 0.1, teacher)
    gain_state = adamw(
        gain_master, gain_moment_one, gain_moment_two, owned_gain, clip_factor, 0.0, gain_teacher
    )
    weights, gain_weights = (
        lax.all_gather(matrix_state[0].astype(jnp.bfloat16), "fsdp", axis=0, tiled=True),
        lax.all_gather(gain_state[0].astype(jnp.bfloat16), "fsdp", axis=0, tiled=True),
    )
    return (
        weights,
        gain_weights,
        matrix_state[0],
        matrix_state[1],
        matrix_state[2],
        matrix_state[3],
        gain_state[0],
        gain_state[1],
        gain_state[2],
        gain_state[3],
    )


def solution(mesh):
    return jax.shard_map(
        shards,
        mesh=mesh,
        in_specs=(
            P("dp", "fsdp", None, "tensor"),
            P("dp", "fsdp", "tensor", None),
            P("fsdp", "tensor"),
            P("fsdp", "tensor"),
            P("fsdp", "tensor"),
            P("fsdp", "tensor"),
            P("fsdp"),
            P("fsdp"),
            P("fsdp"),
            P("fsdp"),
        ),
        out_specs=(
            P(None, "tensor"),
            P(),
            P("fsdp", "tensor"),
            P("fsdp", "tensor"),
            P("fsdp", "tensor"),
            P("fsdp", "tensor"),
            P("fsdp"),
            P("fsdp"),
            P("fsdp"),
            P("fsdp"),
        ),
        check_vma=False,
    )
```

profile of v0, /device:TPU:2, one launch (start us, length us, event | category | flops | bytes accessed | tf_op | source)
XLA Modules:
  0.0 377.3 jit_solution(621989605081140635)
XLA Ops:
  7.2 0.0 copy-start.5
  7.2 0.0 copy-start.2
  7.2 0.0 copy-start.3
  7.2 0.0 copy-start.4
  7.2 0.0 copy-start.1
  7.2 0.0 reduce-scatter.2.cloned.1.call-start
  7.3 2.9 bitcast_convert_fusion
  10.1 0.0 copy-start.6
  10.1 0.0 copy-start.7
  10.1 0.0 copy-start.8
  10.1 0.0 copy-start.9
  10.1 0.0 reduce-scatter.2.cloned.1.call-update
  10.2 0.0 all-reduce.3.cloned.1.call-start
  10.2 78.5 %reduce-scatter.2.cloned.1.call-done = f32[128,256]{1,0:T(8,128)} async-done(((f32[2048,256]{1,0:T(8,128)}), f32[128,256]{1,0:T(8,128)}) %reduce-scatter.2.cloned.1.call-update) | async-done | bytes 131088 | tf_op jit(solution)/shard_map/reduce_scatter | solution.py:51
  88.7 0.0 all-reduce.3.cloned.1.call-update
  88.7 0.0 all-gather.3.cloned.1.call-start
  88.8 0.0 copy-done.5
  88.8 1.3 dynamic-slice
  90.7 28.9 %all-reduce = f32[2048]{0:T(1024)S(1)} all-reduce(f32[2048]{0:T(1024)S(1)} %bitcast.8), channel_id=3, replica_groups=mesh['dp'=8,'fsdp'=16,'tensor'=4] {'fsdp'}, use_global_device_ids=true, to_apply=%region_4.0.clone | all-reduce | flops 2048 | bytes 16384
  119.6 0.1 dynamic-slice.1
  119.7 6.0 %psum.32 = f32[128]{0:T(128)S(1)} all-reduce(f32[128]{0:T(128)S(1)} %dynamic-slice.1), channel_id=1, replica_groups=mesh['dp'=8,'fsdp'=16,'tensor'=4] {'tensor'}, use_global_device_ids=true, to_apply=%region_3.0 | all-reduce | flops 128 | bytes 1024 | tf_op jit(solution)/shard_map/psum | solution.py:48
  125.7 22.9 %psum.30 = f32[128]{0:T(128)S(1)} all-reduce(f32[128]{0:T(128)S(1)} %psum.32), channel_id=1, replica_groups=mesh['dp'=8,'fsdp'=16,'tensor'=4] {'dp'}, use_global_device_ids=true, to_apply=%region_5.0 | all-reduce | flops 128 | bytes 1024 | tf_op jit(solution)/shard_map/psum | solution.py:54
  148.6 0.6 multiply_reduce_fusion.1
  149.8 38.0 %all-reduce.3.cloned.1.call-done = f32[128,256]{1,0:T(8,128)} async-done(((f32[128,256]{1,0:T(8,128)}), f32[128,256]{1,0:T(8,128)}) %all-reduce.3.cloned.1.call-update) | async-done | bytes 131088 | tf_op jit(solution)/shard_map/psum | solution.py:54
  187.8 1.5 multiply_reduce_fusion
  190.0 102.3 %psum.31 = f32[]{:T(128)} all-reduce(f32[]{:T(128)S(6)} %add.54), channel_id=1, replica_groups=mesh['dp'=8,'fsdp'=16,'tensor'=4] {'fsdp','tensor'}, use_global_device_ids=true, to_apply=%region_7.0 | all-reduce | flops 1 | bytes 8 | tf_op jit(solution)/shard_map/psum | solution.py:56
  293.0 0.0 copy-done.2
  293.0 0.0 copy-done.3
  293.0 0.0 copy-done.4
  293.0 0.0 copy-done.1
  293.0 1.7 multiply_add_fusion
  294.7 0.0 copy-start
  294.7 0.7 convert_element_type.22
  295.4 0.0 all-gather.3.cloned.1.call-update
  295.4 0.0 copy-done.6
  295.4 0.0 copy-done.7
  295.5 0.0 copy-done.8
  295.5 0.0 copy-done.9
  295.5 0.5 multiply_add_fusion.2
  296.0 0.0 copy-start.10
  296.0 29.8 %all-gather = bf16[16,1,128]{2,1,0:T(2,128)(2,1)S(1)} all-gather(bf16[1,1,128]{2,1,0:T(2,128)(2,1)S(1)} %convert_bitcast_fusion), channel_id=1, replica_groups=mesh['dp'=8,'fsdp'=16,'tensor'=4] {'fsdp'}, dimensions={0}, use_global_device_ids=true | all-gather | bytes 4352 | tf_op jit(solution)/shard_map/all_gather | solution.py:65
  325.8 0.6 reduce
  326.5 42.0 %all-gather.3.cloned.1.call-done = bf16[2048,256]{1,0:T(8,128)(2,1)} async-done(((bf16[128,256]{1,0:T(8,128)(2,1)}), bf16[2048,256]{1,0:T(8,128)(2,1)}) %all-gather.3.cloned.1.call-update) | async-done | bytes 1048592 | tf_op jit(solution)/shard_map/all_gather | solution.py:64
  368.5 2.3 copy.22
  370.8 0.0 copy-done
  370.8 0.0 copy-done.10
  (2 shorter events, 0.0 us)
Async XLA Ops:
  7.2 81.6 %copy-start.5 = (bf16[1,1,1,2048]{3,2,1,0:T(2,128)(2,1)S(1)}, bf16[1,1,1,2048]{3,2,1,0:T(2,128)(2,1)}, u32[]{:S(2)}) copy-start(bf16[1,1,1,2048]{3,2,1,0:T(2,128)(2,1)} %param.11) | copy-start | bytes 12292
  7.2 285.8 %copy-start.2 = (f32[128,256]{1,0:T(8,128)S(1)}, f32[128,256]{1,0:T(8,128)}, u32[]{:S(2)}) copy-start(f32[128,256]{1,0:T(8,128)} %param.12) | copy-start | bytes 393220
  7.2 285.8 %copy-start.3 = (f32[128,256]{1,0:T(8,128)S(1)}, f32[128,256]{1,0:T(8,128)}, u32[]{:S(2)}) copy-start(f32[128,256]{1,0:T(8,128)} %param.13) | copy-start | bytes 393220
  7.2 285.8 %copy-start.4 = (f32[128,256]{1,0:T(8,128)S(1)}, f32[128,256]{1,0:T(8,128)}, u32[]{:S(2)}) copy-start(f32[128,256]{1,0:T(8,128)} %param.14) | copy-start | bytes 393220
  7.2 285.8 %copy-start.1 = (f32[128,256]{1,0:T(8,128)S(1)}, f32[128,256]{1,0:T(8,128)}, u32[]{:S(2)}) copy-start(f32[128,256]{1,0:T(8,128)} %param.15) | copy-start | bytes 393220
  7.2 81.5 %reduce-scatter.2.cloned.1.call-start = ((), (), s32[]{:S(2)}) async-start(), calls=%async_computation.1 | async-start | bytes 2228224 | tf_op jit(solution)/shard_map/reduce_scatter | solution.py:51
  10.1 285.3 %copy-start.6 = (f32[128]{0:T(128)S(1)}, f32[128]{0:T(128)}, u32[]{:S(2)}) copy-start(f32[128]{0:T(128)} %param.19) | copy-start | bytes 1540
  10.1 285.3 %copy-start.7 = (f32[128]{0:T(128)S(1)}, f32[128]{0:T(128)}, u32[]{:S(2)}) copy-start(f32[128]{0:T(128)} %param.16) | copy-start | bytes 1540
  10.1 285.3 %copy-start.8 = (f32[128]{0:T(128)S(1)}, f32[128]{0:T(128)}, u32[]{:S(2)}) copy-start(f32[128]{0:T(128)} %param.17) | copy-start | bytes 1540
  10.1 285.3 %copy-start.9 = (f32[128]{0:T(128)S(1)}, f32[128]{0:T(128)}, u32[]{:S(2)}) copy-start(f32[128]{0:T(128)} %param.18) | copy-start | bytes 1540
  10.2 177.6 %all-reduce.3.cloned.1.call-start = ((), (), s32[]{:S(2)}) async-start(), calls=%async_computation.2 | async-start | bytes 262144 | tf_op jit(solution)/shard_map/psum | solution.py:54
  88.7 279.8 %all-gather.3.cloned.1.call-start = ((), (), s32[]{:S(2)}) async-start(), calls=%async_computation.3 | async-start | bytes 1114112 | tf_op jit(solution)/shard_map/all_gather | solution.py:64
  294.7 76.1 %copy-start = (f32[128,256]{1,0:T(8,128)}, f32[128,256]{1,0:T(8,128)S(1)}, u32[]{:S(2)}) copy-start(f32[128,256]{1,0:T(8,128)S(1)} %get-tuple-element.30) | copy-start | bytes 393220
  296.0 74.8 %copy-start.10 = (f32[128]{0:T(128)}, f32[128]{0:T(128)S(1)}, u32[]{:S(2)}) copy-start(f32[128]{0:T(128)S(1)} %get-tuple-element.34) | copy-start | bytes 1540
Sparse Core Ops, SparseCore 0:
  10.9 77.7 reduce-scatter.1
  91.6 96.1 all-reduce.2
  295.6 72.9 all-gather.2
where the time goes:
time: 378 us; the launch traced here: 377 us
  blocking collectives  190 us (50%)
  waiting for transfers between devices  159 us (42%)
  between operations  16.6 us (4%)
  other arithmetic  8.58 us (2%)
    psum x1, blocking collectives, shards(): total_squares = lax.psum(own_squares, ('fsdp', 'tensor'))  102 us
    reduce_scatter x1, waiting for transfers between devices, shards(): lax.psum_scatter(local_grad, 'fsdp', scatter_dimension=0, tiled=True)  78.5 us
    all_gather x1, waiting for transfers between devices, shards(): lax.all_gather(matrix_state[0].astype(jnp.bfloat16), 'fsdp', axis=0, tile...  42 us
    psum x1, waiting for transfers between devices, shards(): owned_rows, owned_gain = lax.psum((owned_rows, owned_gain), 'dp')  38 us
    all_gather x1, blocking collectives, shards(): lax.all_gather(gain_state[0].astype(jnp.bfloat16), 'fsdp', axis=0, tiled=...  29.8 us
    unnamed x1, blocking collectives  28.9 us
    psum x1, blocking collectives, shards(): owned_rows, owned_gain = lax.psum((owned_rows, owned_gain), 'dp')  22.9 us
  transfers between devices with their start and end apart: 3, of which 3 were waited for; matrix products, arithmetic and copies ran while one was open for 1% of the time, Pallas kernels for 0%

commit v1 on v0

--- a/solution.py
+++ b/solution.py
@@ -31,6 +31,14 @@
     return (parameter_new, first_new, second_new, shadow_new)
 
 
+def exchange(blocks, axis):
+    return lax.all_to_all(blocks, axis, 0, 0, tiled=True)
+
+
+def to_all(block, count, axis):
+    return exchange(jnp.broadcast_to(block[None], (count, *block.shape)), axis)
+
+
 def shards(
     grad_part,
     gain_grad_part,
@@ -43,27 +51,57 @@
     gain_moment_two,
     gain_teacher,
 ):
-    tensor_count = lax.axis_size("tensor")
-    local_gain = gain_grad_part[0, 0, 0].astype(jnp.float32)
-    local_gain = lax.psum(local_gain, "tensor")
-    local_grad = grad_part[0, 0].astype(jnp.float32)
-    owned_rows, owned_gain = (
-        lax.psum_scatter(local_grad, "fsdp", scatter_dimension=0, tiled=True),
-        lax.psum_scatter(local_gain, "fsdp", scatter_dimension=0, tiled=True),
-    )
-    owned_rows, owned_gain = lax.psum((owned_rows, owned_gain), "dp")
-    own_squares = jnp.sum(owned_rows * owned_rows) + jnp.sum(owned_gain * owned_gain) / tensor_count
-    total_squares = lax.psum(own_squares, ("fsdp", "tensor"))
+    n_dp, n_fsdp = lax.axis_size("dp"), lax.axis_size("fsdp")
+    rows, cols = grad_part.shape[2:]
+    piece = rows // (n_dp * n_fsdp)
+    lines = piece * cols // 128
+
+    with jax.named_scope("sum_dp"):
+        pieces = grad_part.reshape(n_fsdp, n_dp, piece, cols).transpose(1, 0, 2, 3)
+        pieces = pieces.reshape(n_dp, n_fsdp * piece, cols)
+        gain_pieces = gain_grad_part.reshape(n_fsdp, n_dp, piece).transpose(1, 0, 2)
+        gain_pieces = gain_pieces.reshape(n_dp, 1, n_fsdp * piece)
+        gain_pieces = jnp.pad(gain_pieces, ((0, 0), (0, 7), (0, 0)))
+        got = exchange(jnp.concatenate([pieces, gain_pieces], axis=1), "dp")
+        summed = jnp.sum(got.astype(jnp.float32), axis=0)
+    with jax.named_scope("sum_fsdp"):
+        part = summed[: n_fsdp * piece].reshape(n_fsdp, lines, 128)
+        gain_part = summed[n_fsdp * piece].reshape(n_fsdp, 1, piece)
+        gain_part = jnp.pad(gain_part, ((0, 0), (0, 7), (0, 128 - piece)))
+        got = exchange(jnp.concatenate([part, gain_part], axis=1), "fsdp")
+        summed = jnp.sum(got, axis=0)
+        own, own_gain = summed[:lines], summed[lines]
+    with jax.named_scope("sum_tensor"):
+        own_squares = jnp.sum(own * own)
+        lane = lax.iota(jnp.int32, 128)
+        total = lax.psum(jnp.where(lane == piece, own_squares, own_gain), "tensor")
+        gain_piece = jnp.where(lane < piece, total, 0.0)
+        squares = total[piece] + jnp.sum(gain_piece * gain_piece)
+        line = jnp.where(lane == piece, squares, gain_piece)
+    with jax.named_scope("share_dp"):
+        block = jnp.concatenate([own, jnp.pad(line[None], ((0, 7), (0, 0)))], axis=0)
+        got = to_all(block, n_dp, "dp")
+        owned_rows = got[:, :lines].reshape(n_dp * piece, cols)
+        owned_gain = got[:, lines, :piece].reshape(n_dp * piece)
+        squares = jnp.sum(got[:, lines, piece])
+    with jax.named_scope("squares_fsdp"):
+        got = to_all(jnp.full((1, 128), squares), n_fsdp, "fsdp")
+        total_squares = jnp.sum(got[:, 0, 0])
     clip_limit = clip_level * math.sqrt(D * HEADS * HEAD + D)
     clip_factor = clip_limit / (jnp.sqrt(total_squares) + 1e-06)
     matrix_state = adamw(master, moment_one, moment_two, owned_rows, clip_factor, 0.1, teacher)
     gain_state = adamw(
         gain_master, gain_moment_one, gain_moment_two, owned_gain, clip_factor, 0.0, gain_teacher
     )
-    weights, gain_weights = (
-        lax.all_gather(matrix_state[0].astype(jnp.bfloat16), "fsdp", axis=0, tiled=True),
-        lax.all_gather(gain_state[0].astype(jnp.bfloat16), "fsdp", axis=0, tiled=True),
-    )
+    with jax.named_scope("weights_fsdp"):
+        mine = matrix_state[0].astype(jnp.bfloat16).reshape(n_dp, lines, 128)
+        mine = lax.dynamic_index_in_dim(mine, lax.axis_index("dp"), 0, keepdims=False)
+        gain_mine = jnp.pad(gain_state[0].astype(jnp.bfloat16)[None], ((0, 7), (0, 0)))
+        got = to_all(jnp.concatenate([mine, gain_mine], axis=0), n_fsdp, "fsdp")
+        gain_weights = got[:, lines].reshape(rows)
+    with jax.named_scope("weights_dp"):
+        got = to_all(got[:, :lines].reshape(n_fsdp * piece, cols), n_dp, "dp")
+        weights = got.reshape(n_dp, n_fsdp, piece, cols).transpose(1, 0, 2, 3).reshape(rows, cols)
     return (
         weights,
         gain_weights,

time: 378 us -> 141 us (0.37)
  waiting for transfers between devices: 159 us -> 24.5 us
  blocking collectives: 190 us -> 91.5 us
  between operations: 16.6 us -> 2.99 us
  starting transfers between devices: 0.12 us -> 9.53 us
    psum x3 -> x1, blocking collectives: 131 us -> 5.67 us  [shards(): total = lax.psum(jnp.where(lane == piece, own_squares, own_gain), 'tensor')]
    all_to_all x0 -> x4, blocking collectives: none -> 85.8 us  [exchange(): return lax.all_to_all(blocks, axis, 0, 0, tiled=True)]
    reduce_scatter x1 -> x0, waiting for transfers between devices: 78.5 us -> none  [shards(): lax.psum_scatter(local_grad, 'fsdp', scatter_dimension=0, tiled=True)]
    all_gather x1 -> x0, waiting for transfers between devices: 42 us -> none  [shards(): lax.all_gather(matrix_state[0].astype(jnp.bfloat16), 'fsdp', axis=0, tile...]
    psum x1 -> x0, waiting for transfers between devices: 38 us -> none  [shards(): owned_rows, owned_gain = lax.psum((owned_rows, owned_gain), 'dp')]
    all_gather x1 -> x0, blocking collectives: 29.8 us -> none  [shards(): lax.all_gather(gain_state[0].astype(jnp.bfloat16), 'fsdp', axis=0, tiled=...]
    unnamed x1 -> x0, blocking collectives: 28.9 us -> none
    all_to_all x0 -> x2, waiting for transfers between devices: none -> 24.5 us  [exchange(): return lax.all_to_all(blocks, axis, 0, 0, tiled=True)]
  transfers between devices with their start and end apart: 3 -> 2, of which waited for: 3 -> 2; matrix products, arithmetic and copies ran while one was open for 1% -> 0% of each run, Pallas kernels for 0% -> 0%
where the time goes in v1:
time: 141 us
  blocking collectives  91.5 us (65%)
  waiting for transfers between devices  24.5 us (17%)
  starting transfers between devices  9.53 us (7%)
  local copies, waits for them, and re-layouts  6.51 us (5%)
  other arithmetic  5.57 us (4%)
  between operations  2.99 us (2%)
    all_to_all x4, blocking collectives, exchange(): return lax.all_to_all(blocks, axis, 0, 0, tiled=True)  85.8 us
    all_to_all x2, waiting for transfers between devices, exchange(): return lax.all_to_all(blocks, axis, 0, 0, tiled=True)  24.5 us
    all_to_all x2, starting transfers between devices, exchange(): return lax.all_to_all(blocks, axis, 0, 0, tiled=True)  9.53 us
    psum x1, blocking collectives, shards(): total = lax.psum(jnp.where(lane == piece, own_squares, own_gain), 'tensor')  5.67 us
  transfers between devices with their start and end apart: 2, of which 2 were waited for; matrix products, arithmetic and copies ran while one was open for 0% of the time, Pallas kernels for 0%

profile of v1, /device:TPU:2, one launch (start us, length us, event | category | flops | bytes accessed | tf_op | source)
XLA Modules:
  0.0 140.5 jit_solution(18431092805480685050)
XLA Ops:
  0.6 0.7 reduce.2
  1.4 0.1 reshape.55
  1.5 0.1 reshape.61
  1.6 1.3 copy.44
  2.9 0.1 fusion.1
  3.0 23.7 %all_to_all.30 = bf16[8,264,256]{2,1,0:T(8,128)(2,1)S(1)} all-to-all(bf16[8,264,256]{2,1,0:T(8,128)(2,1)S(1)} %fusion.1), channel_id=1, replica_groups=mesh['dp'=8,'fsdp'=16,'tensor'=4] {'dp'}, dimensions={0} | all-to-all | bytes 2162688 | tf_op jit(solution)/shard_map/sum_dp/all_to_all | solution.py:35
  26.7 0.1 convert_reduce_fusion
  26.9 0.1 squeeze.19
  27.0 0.0 copy-start.5
  27.0 0.0 copy-start.6
  27.0 0.0 copy-start.7
  27.0 0.0 copy-start.8
  27.0 0.0 copy-start.1
  27.1 0.0 copy-start.2
  27.1 0.0 copy-start.3
  27.1 0.0 copy-start.4
  27.1 34.5 %all_to_all.31 = f32[16,40,128]{2,1,0:T(8,128)S(1)} all-to-all(f32[16,40,128]{2,1,0:T(8,128)S(1)} %select_maximum_fusion), channel_id=1, replica_groups=mesh['dp'=8,'fsdp'=16,'tensor'=4] {'fsdp'}, dimensions={0} | all-to-all | bytes 655360 | tf_op jit(solution)/shard_map/sum_fsdp/all_to_all | solution.py:35
  61.7 0.6 fusion.10
  62.3 0.6 compare_select_fusion.2
  62.9 5.7 %psum.7 = f32[128]{0:T(128)S(1)} all-reduce(f32[128]{0:T(128)S(1)} %compare_select_fusion.2), channel_id=1, replica_groups=mesh['dp'=8,'fsdp'=16,'tensor'=4] {'tensor'}, use_global_device_ids=true, to_apply=%region_3.4 | all-reduce | flops 128 | bytes 1024 | tf_op jit(solution)/shard_map/sum_tensor/psum | solution.py:77
  68.6 0.6 multiply_reduce_fusion.1
  69.2 0.6 slice.37
  71.1 11.6 %all_to_all.32 = f32[8,40,128]{2,1,0:T(8,128)S(1)} all-to-all(f32[8,40,128]{2,1,0:T(8,128)S(1)} %broadcast_in_dim.43), channel_id=1, replica_groups=mesh['dp'=8,'fsdp'=16,'tensor'=4] {'dp'}, dimensions={0} | all-to-all | bytes 327680 | tf_op jit(solution)/shard_map/share_dp/all_to_all | solution.py:35
  82.7 0.7 slice_reduce_fusion.1
  83.4 1.2 broadcast_in_dim.44
  84.7 6.0 %all-to-all-start.3 = ((f32[16,1,128]{2,1,0:T(1,128)}), f32[16,1,128]{2,1,0:T(1,128)S(1)}, u32[]{:S(2)}, u32[]{:S(2)}) async-start(f32[16,1,128]{2,1,0:T(1,128)} %broadcast_in_dim.44), calls=%async_computation.3 | async-start | bytes 16384 | tf_op jit(solution)/shard_map/squares_fsdp/all_to_all | solution.py:35
  90.6 12.4 %all-to-all-done.3 = f32[16,1,128]{2,1,0:T(1,128)S(1)} async-done(((f32[16,1,128]{2,1,0:T(1,128)}), f32[16,1,128]{2,1,0:T(1,128)S(1)}, u32[]{:S(2)}, u32[]{:S(2)}) %all-to-all-start.3) | async-done | bytes 8224 | tf_op jit(solution)/shard_map/squares_fsdp/all_to_all | solution.py:35
  103.0 0.6 slice_reduce_fusion
  104.4 0.1 mul.138
  104.5 0.0 copy-done.5
  104.5 0.0 copy-done.6
  104.5 0.0 copy-done.7
  104.6 0.0 copy-done.8
  104.6 0.5 multiply_add_fusion.2
  105.1 0.0 copy-start.9
  105.1 0.0 copy-done.1
  105.1 0.0 copy-done.2
  105.1 0.0 copy-done.3
  105.1 0.0 copy-done.4
  105.1 0.8 multiply_add_fusion
  106.1 16.0 %all_to_all.33 = bf16[16,40,128]{2,1,0:T(8,128)(2,1)S(1)} all-to-all(bf16[16,40,128]{2,1,0:T(8,128)(2,1)S(1)} %broadcast_in_dim.46), channel_id=1, replica_groups=mesh['dp'=8,'fsdp'=16,'tensor'=4] {'fsdp'}, dimensions={0} | all-to-all | bytes 327680 | tf_op jit(solution)/shard_map/weights_fsdp/all_to_all | solution.py:35
  122.1 0.0 copy-done.9
  122.1 1.0 broadcast_in_dim.48
  123.2 0.0 copy-done
  123.2 3.6 %all-to-all-start.5 = ((bf16[8,256,256]{2,1,0:T(8,128)(2,1)}), bf16[8,256,256]{2,1,0:T(8,128)(2,1)S(1)}, u32[]{:S(2)}, u32[]{:S(2)}) async-start(bf16[8,256,256]{2,1,0:T(8,128)(2,1)} %broadcast_in_dim.48), calls=%async_computation.5 | async-start | bytes 2097152 | tf_op jit(solution)/shard_map/weights_dp/all_to_all | solution.py:35
  126.8 0.6 copy.55
  127.3 12.1 %all-to-all-done.5 = bf16[8,256,256]{2,1,0:T(8,128)(2,1)S(1)} async-done(((bf16[8,256,256]{2,1,0:T(8,128)(2,1)}), bf16[8,256,256]{2,1,0:T(8,128)(2,1)S(1)}, u32[]{:S(2)}, u32[]{:S(2)}) %all-to-all-start.5) | async-done | bytes 1048608 | tf_op jit(solution)/shard_map/weights_dp/all_to_all | solution.py:35
  139.5 1.1 copy.48
  (22 shorter events, 0.4 us)
Async XLA Ops:
  27.0 77.5 %copy-start.5 = (f32[128]{0:T(128)S(1)}, f32[128]{0:T(128)}, u32[]{:S(2)}) copy-start(f32[128]{0:T(128)} %param.19) | copy-start | bytes 1540
  27.0 77.5 %copy-start.6 = (f32[128]{0:T(128)S(1)}, f32[128]{0:T(128)}, u32[]{:S(2)}) copy-start(f32[128]{0:T(128)} %param.16) | copy-start | bytes 1540
  27.0 77.5 %copy-start.7 = (f32[128]{0:T(128)S(1)}, f32[128]{0:T(128)}, u32[]{:S(2)}) copy-start(f32[128]{0:T(128)} %param.17) | copy-start | bytes 1540
  27.0 77.5 %copy-start.8 = (f32[128]{0:T(128)S(1)}, f32[128]{0:T(128)}, u32[]{:S(2)}) copy-start(f32[128]{0:T(128)} %param.18) | copy-start | bytes 1540
  27.0 78.1 %copy-start.1 = (f32[128,256]{1,0:T(8,128)S(1)}, f32[128,256]{1,0:T(8,128)}, u32[]{:S(2)}) copy-start(f32[128,256]{1,0:T(8,128)} %param.15) | copy-start | bytes 393220
  27.1 78.1 %copy-start.2 = (f32[128,256]{1,0:T(8,128)S(1)}, f32[128,256]{1,0:T(8,128)}, u32[]{:S(2)}) copy-start(f32[128,256]{1,0:T(8,128)} %param.12) | copy-start | bytes 393220
  27.1 78.1 %copy-start.3 = (f32[128,256]{1,0:T(8,128)S(1)}, f32[128,256]{1,0:T(8,128)}, u32[]{:S(2)}) copy-start(f32[128,256]{1,0:T(8,128)} %param.13) | copy-start | bytes 393220
  27.1 78.1 %copy-start.4 = (f32[128,256]{1,0:T(8,128)S(1)}, f32[128,256]{1,0:T(8,128)}, u32[]{:S(2)}) copy-start(f32[128,256]{1,0:T(8,128)} %param.14) | copy-start | bytes 393220
  84.7 18.4 %all-to-all-start.3 = ((f32[16,1,128]{2,1,0:T(1,128)}), f32[16,1,128]{2,1,0:T(1,128)S(1)}, u32[]{:S(2)}, u32[]{:S(2)}) async-start(f32[16,1,128]{2,1,0:T(1,128)} %broadcast_in_dim.44), calls=%async_computation.3 | async-start | bytes 16384 | tf_op jit(solution)/shard_map/squares_fsdp/all_to_all | solution.py:35
  105.1 17.0 %copy-start.9 = (f32[128]{0:T(128)}, f32[128]{0:T(128)S(1)}, u32[]{:S(2)}) copy-start(f32[128]{0:T(128)S(1)} %get-tuple-element.11) | copy-start | bytes 1540
  106.0 17.2 %copy-start = (f32[128,256]{1,0:T(8,128)}, f32[128,256]{1,0:T(8,128)S(1)}, u32[]{:S(2)}) copy-start(f32[128,256]{1,0:T(8,128)S(1)} %get-tuple-element.15) | copy-start | bytes 393220
  123.2 16.3 %all-to-all-start.5 = ((bf16[8,256,256]{2,1,0:T(8,128)(2,1)}), bf16[8,256,256]{2,1,0:T(8,128)(2,1)S(1)}, u32[]{:S(2)}, u32[]{:S(2)}) async-start(bf16[8,256,256]{2,1,0:T(8,128)(2,1)} %broadcast_in_dim.48), calls=%async_computation.5 | async-start | bytes 2097152 | tf_op jit(solution)/shard_map/weights_dp/all_to_all | solution.py:35

commit v2 on v0

--- a/solution.py
+++ b/solution.py
@@ -31,6 +31,14 @@
     return (parameter_new, first_new, second_new, shadow_new)
 
 
+def exchange(blocks, axis):
+    return lax.all_to_all(blocks, axis, 0, 0, tiled=True)
+
+
+def to_all(block, count, axis):
+    return exchange(jnp.broadcast_to(block[None], (count, *block.shape)), axis)
+
+
 def shards(
     grad_part,
     gain_grad_part,
@@ -43,38 +51,67 @@
     gain_moment_two,
     gain_teacher,
 ):
-    tensor_count = lax.axis_size("tensor")
-    local_gain = gain_grad_part[0, 0, 0].astype(jnp.float32)
-    local_gain = lax.psum(local_gain, "tensor")
-    local_grad = grad_part[0, 0].astype(jnp.float32)
-    owned_rows, owned_gain = (
-        lax.psum_scatter(local_grad, "fsdp", scatter_dimension=0, tiled=True),
-        lax.psum_scatter(local_gain, "fsdp", scatter_dimension=0, tiled=True),
-    )
-    owned_rows, owned_gain = lax.psum((owned_rows, owned_gain), "dp")
-    own_squares = jnp.sum(owned_rows * owned_rows) + jnp.sum(owned_gain * owned_gain) / tensor_count
-    total_squares = lax.psum(own_squares, ("fsdp", "tensor"))
+    n_dp, n_fsdp, n_tensor = (lax.axis_size(a) for a in ("dp", "fsdp", "tensor"))
+    rows, cols = grad_part.shape[2:]
+    block = rows // n_fsdp
+    piece = block // n_dp
+    lines = piece * cols // 128
+    halves = cols // 128
+
+    with jax.named_scope("sum_dp"):
+        pieces = grad_part.reshape(n_fsdp, n_dp, piece, cols).transpose(1, 0, 2, 3)
+        pieces = pieces.reshape(n_dp, n_fsdp * piece, cols)
+        gain_rows = gain_grad_part.reshape(1, rows // cols, cols)
+        gain_rows = jnp.broadcast_to(gain_rows, (n_dp, *gain_rows.shape[1:]))
+        got = exchange(jnp.concatenate([pieces, gain_rows], axis=1), "dp")
+        summed = jnp.sum(got.astype(jnp.float32), axis=0)
+    with jax.named_scope("sum_fsdp"):
+        part = summed[: n_fsdp * piece].reshape(n_fsdp, piece, cols)
+        part = [part[:, :, 128 * h : 128 * (h + 1)] for h in range(halves)]
+        gain_part = summed[n_fsdp * piece :].reshape(n_fsdp, 1, block)
+        got = exchange(jnp.concatenate([*part, gain_part], axis=1), "fsdp")
+        summed = jnp.sum(got, axis=0)
+        own, own_gain = summed[:lines], summed[lines:]
+        own_squares = jnp.sum(own * own, axis=0, keepdims=True)
+    with jax.named_scope("squares_dp_tensor"):
+        line = jnp.concatenate([own_gain, own_squares], axis=1)
+        got = to_all(line, n_dp * n_tensor, ("dp", "tensor"))
+        owned_gain = jnp.sum(got[:n_tensor, 0, :block], axis=0)
+        squares = jnp.sum(got[:, 0, block:], axis=0) + owned_gain * owned_gain
+    with jax.named_scope("squares_fsdp"):
+        total_squares = jnp.sum(to_all(squares[None], n_fsdp, "fsdp"))
     clip_limit = clip_level * math.sqrt(D * HEADS * HEAD + D)
     clip_factor = clip_limit / (jnp.sqrt(total_squares) + 1e-06)
-    matrix_state = adamw(master, moment_one, moment_two, owned_rows, clip_factor, 0.1, teacher)
     gain_state = adamw(
         gain_master, gain_moment_one, gain_moment_two, owned_gain, clip_factor, 0.0, gain_teacher
     )
-    weights, gain_weights = (
-        lax.all_gather(matrix_state[0].astype(jnp.bfloat16), "fsdp", axis=0, tiled=True),
-        lax.all_gather(gain_state[0].astype(jnp.bfloat16), "fsdp", axis=0, tiled=True),
-    )
+    with jax.named_scope("weights_fsdp"):
+        own = jnp.concatenate([own[piece * h : piece * (h + 1)] for h in range(halves)], axis=1)
+        high = lax.reduce_precision(own, 8, 7)
+        low = lax.reduce_precision(own - high, 8, 7)
+        first = lax.axis_index("dp") * piece
+        state = [lax.dynamic_slice_in_dim(a, first, piece) for a in (master, moment_one, moment_two)]
+        mine = adamw(*state, high + low, clip_factor, 0.1, jnp.float32(0))[0].astype(jnp.bfloat16)
+        gain_mine = jnp.pad(gain_state[0].astype(jnp.bfloat16)[None], ((0, 0), (0, cols - block)))
+        got = to_all(jnp.concatenate([mine, gain_mine], axis=0), n_fsdp, "fsdp")
+        gain_weights = got[:, piece, :block].reshape(rows)
+    with jax.named_scope("weights_dp"):
+        mine = got[:, :piece].reshape(n_fsdp * piece, cols)
+        terms = [t.astype(jnp.bfloat16) for t in (high, low)]
+        got = to_all(jnp.concatenate([mine, *terms], axis=0), n_dp, "dp")
+        weights = got[:, : n_fsdp * piece].reshape(n_dp, n_fsdp, piece, cols)
+        weights = weights.transpose(1, 0, 2, 3).reshape(rows, cols)
+        high, low = (
+            got[:, (n_fsdp + i) * piece : (n_fsdp + i + 1) * piece].reshape(block, cols)
+            for i in range(2)
+        )
+        owned_rows = high.astype(jnp.float32) + low.astype(jnp.float32)
+    matrix_state = adamw(master, moment_one, moment_two, owned_rows, clip_factor, 0.1, teacher)
     return (
         weights,
         gain_weights,
-        matrix_state[0],
-        matrix_state[1],
-        matrix_state[2],
-        matrix_state[3],
-        gain_state[0],
-        gain_state[1],
-        gain_state[2],
-        gain_state[3],
+        *matrix_state,
+        *gain_state,
     )
 
 

time: 378 us -> 135 us (0.36)
  the two profiles are of different devices: /device:TPU:2 before, /device:TPU:32 now
where the time goes in v2:
time: 135 us; the launch traced here: 134 us
  blocking collectives  77.6 us (57%)
  waiting for transfers between devices  31.9 us (24%)
  starting transfers between devices  14.2 us (11%)
  local copies, waits for them, and re-layouts  5.58 us (4%)
  other arithmetic  3.16 us (2%)
  between operations  1.65 us (1%)
    all_to_all x3, blocking collectives, exchange(): return lax.all_to_all(blocks, axis, 0, 0, tiled=True)  77.6 us
    all_to_all x3, waiting for transfers between devices, exchange(): return lax.all_to_all(blocks, axis, 0, 0, tiled=True)  31.9 us
    all_to_all x3, starting transfers between devices, exchange(): return lax.all_to_all(blocks, axis, 0, 0, tiled=True)  14.2 us
  transfers between devices with their start and end apart: 3, of which 3 were waited for; matrix products, arithmetic and copies ran while one was open for 0% of the time, Pallas kernels for 0%

profile of v2, /device:TPU:32, one launch (start us, length us, event | category | flops | bytes accessed | tf_op | source)
XLA Modules:
  0.0 134.1 jit_solution(12713280523125827400)
XLA Ops:
  0.6 0.7 reduce.2
  1.4 1.3 copy.32
  2.7 0.1 pad_maximum_fusion
  2.8 24.5 %all_to_all.30 = bf16[8,264,256]{2,1,0:T(8,128)(2,1)S(1)} all-to-all(bf16[8,264,256]{2,1,0:T(8,128)(2,1)S(1)} %pad_maximum_fusion), channel_id=1, replica_groups=mesh['dp'=8,'fsdp'=16,'tensor'=4] {'dp'}, dimensions={0} | all-to-all | bytes 2162688 | tf_op jit(solution)/shard_map/sum_dp/all_to_all | solution.py:35
  27.3 0.1 convert_reduce_fusion
  27.5 0.0 copy-start.4
  27.5 0.0 copy-start.5
  27.5 0.0 copy-start.6
  27.5 0.0 copy-start.7
  27.5 0.0 copy-start
  27.5 0.0 copy-start.1
  27.6 0.0 copy-start.2
  27.6 33.8 %all_to_all.31 = f32[16,33,128]{2,1,0:T(8,128)S(1)} all-to-all(f32[16,33,128]{2,1,0:T(8,128)S(1)} %pad_maximum_fusion.1), channel_id=1, replica_groups=mesh['dp'=8,'fsdp'=16,'tensor'=4] {'fsdp'}, dimensions={0} | all-to-all | bytes 540672 | tf_op jit(solution)/shard_map/sum_fsdp/all_to_all | solution.py:35
  61.5 0.6 broadcast_in_dim.43
  62.1 3.9 %all-to-all-start.2 = ((f32[32,1,256]{2,1,0:T(1,128)}), f32[32,1,256]{2,1,0:T(1,128)S(1)}, u32[]{:S(2)}, u32[]{:S(2)}) async-start(f32[32,1,256]{2,1,0:T(1,128)} %broadcast_in_dim.43), calls=%async_computation.2 | async-start | bytes 65536 | tf_op jit(solution)/shard_map/squares_dp_tensor/all_to_all | solution.py:35
  66.0 7.5 %all-to-all-done.2 = f32[32,1,256]{2,1,0:T(1,128)S(1)} async-done(((f32[32,1,256]{2,1,0:T(1,128)}), f32[32,1,256]{2,1,0:T(1,128)S(1)}, u32[]{:S(2)}, u32[]{:S(2)}) %all-to-all-start.2) | async-done | bytes 32800 | tf_op jit(solution)/shard_map/squares_dp_tensor/all_to_all | solution.py:35
  73.6 0.6 broadcast_in_dim.44
  74.2 6.8 %all-to-all-start.3 = ((f32[16,1,128]{2,1,0:T(1,128)}), f32[16,1,128]{2,1,0:T(1,128)S(1)}, u32[]{:S(2)}, u32[]{:S(2)}) async-start(f32[16,1,128]{2,1,0:T(1,128)} %broadcast_in_dim.44), calls=%async_computation.3 | async-start | bytes 16384 | tf_op jit(solution)/shard_map/squares_fsdp/all_to_all | solution.py:35
  80.9 11.0 %all-to-all-done.3 = f32[16,1,128]{2,1,0:T(1,128)S(1)} async-done(((f32[16,1,128]{2,1,0:T(1,128)}), f32[16,1,128]{2,1,0:T(1,128)S(1)}, u32[]{:S(2)}, u32[]{:S(2)}) %all-to-all-start.3) | async-done | bytes 8224 | tf_op jit(solution)/shard_map/squares_fsdp/all_to_all | solution.py:35
  92.0 0.6 reduce_sum.59
  93.3 0.0 copy-done.4
  93.3 0.0 copy-done.5
  93.3 0.0 copy-done.6
  93.3 0.0 copy-done.7
  93.3 0.5 multiply_add_fusion.1
  93.9 0.0 copy-start.8
  93.9 0.0 copy-done
  93.9 0.0 copy-done.1
  93.9 0.0 copy-done.2
  94.0 19.4 %all_to_all.32 = bf16[16,17,256]{2,1,0:T(8,128)(2,1)S(1)} all-to-all(bf16[16,17,256]{2,1,0:T(8,128)(2,1)S(1)} %broadcast_in_dim.46), channel_id=1, replica_groups=mesh['dp'=8,'fsdp'=16,'tensor'=4] {'fsdp'}, dimensions={0} | all-to-all | bytes 278528 | tf_op jit(solution)/shard_map/weights_fsdp/all_to_all | solution.py:35
  113.4 1.1 broadcast_in_dim.47
  114.5 0.0 copy-done.8
  114.5 3.6 %all-to-all-start.5 = ((bf16[8,288,256]{2,1,0:T(8,128)(2,1)}), bf16[8,288,256]{2,1,0:T(8,128)(2,1)S(1)}, u32[]{:S(2)}, u32[]{:S(2)}) async-start(bf16[8,288,256]{2,1,0:T(8,128)(2,1)} %broadcast_in_dim.47), calls=%async_computation.5 | async-start | bytes 2359296 | tf_op jit(solution)/shard_map/weights_dp/all_to_all | solution.py:35
  118.1 0.6 slice_reduce_fusion
  118.7 13.4 %all-to-all-done.5 = bf16[8,288,256]{2,1,0:T(8,128)(2,1)S(1)} async-done(((bf16[8,288,256]{2,1,0:T(8,128)(2,1)}), bf16[8,288,256]{2,1,0:T(8,128)(2,1)S(1)}, u32[]{:S(2)}, u32[]{:S(2)}) %all-to-all-start.5) | async-done | bytes 1179680 | tf_op jit(solution)/shard_map/weights_dp/all_to_all | solution.py:35
  132.1 0.1 slice.73
  132.1 0.0 copy-start.3
  132.1 1.1 copy.37
  133.2 0.0 copy-done.3
  133.3 0.9 multiply_add_fusion
  (24 shorter events, 0.3 us)
Async XLA Ops:
  27.5 65.8 %copy-start.4 = (f32[128]{0:T(128)S(1)}, f32[128]{0:T(128)}, u32[]{:S(2)}) copy-start(f32[128]{0:T(128)} %param.19) | copy-start | bytes 1540
  27.5 65.8 %copy-start.5 = (f32[128]{0:T(128)S(1)}, f32[128]{0:T(128)}, u32[]{:S(2)}) copy-start(f32[128]{0:T(128)} %param.16) | copy-start | bytes 1540
  27.5 65.8 %copy-start.6 = (f32[128]{0:T(128)S(1)}, f32[128]{0:T(128)}, u32[]{:S(2)}) copy-start(f32[128]{0:T(128)} %param.17) | copy-start | bytes 1540
  27.5 65.8 %copy-start.7 = (f32[128]{0:T(128)S(1)}, f32[128]{0:T(128)}, u32[]{:S(2)}) copy-start(f32[128]{0:T(128)} %param.18) | copy-start | bytes 1540
  27.5 66.4 %copy-start = (f32[128,256]{1,0:T(8,128)S(1)}, f32[128,256]{1,0:T(8,128)}, u32[]{:S(2)}) copy-start(f32[128,256]{1,0:T(8,128)} %param.14) | copy-start | bytes 393220
  27.5 66.4 %copy-start.1 = (f32[128,256]{1,0:T(8,128)S(1)}, f32[128,256]{1,0:T(8,128)}, u32[]{:S(2)}) copy-start(f32[128,256]{1,0:T(8,128)} %param.13) | copy-start | bytes 393220
  27.6 66.3 %copy-start.2 = (f32[128,256]{1,0:T(8,128)S(1)}, f32[128,256]{1,0:T(8,128)}, u32[]{:S(2)}) copy-start(f32[128,256]{1,0:T(8,128)} %param.12) | copy-start | bytes 393220
  62.1 11.4 %all-to-all-start.2 = ((f32[32,1,256]{2,1,0:T(1,128)}), f32[32,1,256]{2,1,0:T(1,128)S(1)}, u32[]{:S(2)}, u32[]{:S(2)}) async-start(f32[32,1,256]{2,1,0:T(1,128)} %broadcast_in_dim.43), calls=%async_computation.2 | async-start | bytes 65536 | tf_op jit(solution)/shard_map/squares_dp_tensor/all_to_all | solution.py:35
  74.2 17.8 %all-to-all-start.3 = ((f32[16,1,128]{2,1,0:T(1,128)}), f32[16,1,128]{2,1,0:T(1,128)S(1)}, u32[]{:S(2)}, u32[]{:S(2)}) async-start(f32[16,1,128]{2,1,0:T(1,128)} %broadcast_in_dim.44), calls=%async_computation.3 | async-start | bytes 16384 | tf_op jit(solution)/shard_map/squares_fsdp/all_to_all | solution.py:35
  93.9 20.6 %copy-start.8 = (f32[128]{0:T(128)}, f32[128]{0:T(128)S(1)}, u32[]{:S(2)}) copy-start(f32[128]{0:T(128)S(1)} %get-tuple-element.11) | copy-start | bytes 1540
  114.5 17.5 %all-to-all-start.5 = ((bf16[8,288,256]{2,1,0:T(8,128)(2,1)}), bf16[8,288,256]{2,1,0:T(8,128)(2,1)S(1)}, u32[]{:S(2)}, u32[]{:S(2)}) async-start(bf16[8,288,256]{2,1,0:T(8,128)(2,1)} %broadcast_in_dim.47), calls=%async_computation.5 | async-start | bytes 2359296 | tf_op jit(solution)/shard_map/weights_dp/all_to_all | solution.py:35
  132.1 1.1 copy-start.3

commit v3 on v2

--- a/solution.py
+++ b/solution.py
@@ -57,48 +57,60 @@
     piece = block // n_dp
     lines = piece * cols // 128
     halves = cols // 128
+    chunk = rows // n_dp
+    ordered = lax.optimization_barrier
 
     with jax.named_scope("sum_dp"):
         pieces = grad_part.reshape(n_fsdp, n_dp, piece, cols).transpose(1, 0, 2, 3)
         pieces = pieces.reshape(n_dp, n_fsdp * piece, cols)
-        gain_rows = gain_grad_part.reshape(1, rows // cols, cols)
-        gain_rows = jnp.broadcast_to(gain_rows, (n_dp, *gain_rows.shape[1:]))
-        got = exchange(jnp.concatenate([pieces, gain_rows], axis=1), "dp")
+        pieces = jnp.concatenate([pieces, gain_grad_part.reshape(n_dp, chunk // cols, cols)], axis=1)
+        owner, first = lax.axis_index("fsdp") * block, lax.axis_index("dp") * piece
+        owner, first, pieces = ordered((owner, first, pieces))
+        got = exchange(pieces, "dp")
         summed = jnp.sum(got.astype(jnp.float32), axis=0)
     with jax.named_scope("sum_fsdp"):
         part = summed[: n_fsdp * piece].reshape(n_fsdp, piece, cols)
-        part = [part[:, :, 128 * h : 128 * (h + 1)] for h in range(halves)]
-        gain_part = summed[n_fsdp * piece :].reshape(n_fsdp, 1, block)
-        got = exchange(jnp.concatenate([*part, gain_part], axis=1), "fsdp")
-        summed = jnp.sum(got, axis=0)
-        own, own_gain = summed[:lines], summed[lines:]
+        part = jnp.concatenate([part[:, :, 128 * h : 128 * (h + 1)] for h in range(halves)], axis=1)
+        gain_part = summed[n_fsdp * piece :].reshape(1, chunk)
+        part, gain_part = ordered((part, gain_part))
+        own = jnp.sum(exchange(part, "fsdp"), axis=0)
+        own, owner, first = ordered((own, owner, first))
+        state = [lax.dynamic_slice_in_dim(a, first, piece) for a in (master, moment_one, moment_two)]
         own_squares = jnp.sum(own * own, axis=0, keepdims=True)
-    with jax.named_scope("squares_dp_tensor"):
-        line = jnp.concatenate([own_gain, own_squares], axis=1)
-        got = to_all(line, n_dp * n_tensor, ("dp", "tensor"))
-        owned_gain = jnp.sum(got[:n_tensor, 0, :block], axis=0)
-        squares = jnp.sum(got[:, 0, block:], axis=0) + owned_gain * owned_gain
-    with jax.named_scope("squares_fsdp"):
-        total_squares = jnp.sum(to_all(squares[None], n_fsdp, "fsdp"))
-    clip_limit = clip_level * math.sqrt(D * HEADS * HEAD + D)
-    clip_factor = clip_limit / (jnp.sqrt(total_squares) + 1e-06)
-    gain_state = adamw(
-        gain_master, gain_moment_one, gain_moment_two, owned_gain, clip_factor, 0.0, gain_teacher
-    )
-    with jax.named_scope("weights_fsdp"):
         own = jnp.concatenate([own[piece * h : piece * (h + 1)] for h in range(halves)], axis=1)
         high = lax.reduce_precision(own, 8, 7)
         low = lax.reduce_precision(own - high, 8, 7)
-        first = lax.axis_index("dp") * piece
-        state = [lax.dynamic_slice_in_dim(a, first, piece) for a in (master, moment_one, moment_two)]
-        mine = adamw(*state, high + low, clip_factor, 0.1, jnp.float32(0))[0].astype(jnp.bfloat16)
-        gain_mine = jnp.pad(gain_state[0].astype(jnp.bfloat16)[None], ((0, 0), (0, cols - block)))
-        got = to_all(jnp.concatenate([mine, gain_mine], axis=0), n_fsdp, "fsdp")
-        gain_weights = got[:, piece, :block].reshape(rows)
+        own = high + low
+        terms = jnp.concatenate([high.astype(jnp.bfloat16), low.astype(jnp.bfloat16)], axis=0)
+    with jax.named_scope("squares_fsdp"):
+        line = [a[None] for a in (gain_master, gain_moment_one, gain_moment_two)]
+        line = jnp.concatenate([own_squares, gain_part, *line], axis=1)
+        line, own, terms, state, owner = ordered((line, own, terms, state, owner))
+        got = to_all(line, n_fsdp, "fsdp")
+        gain_states = got[:, 0, 128 + chunk :].reshape(n_fsdp, 3, block)
+        line = jnp.sum(got[:, :, : 128 + chunk], axis=0)
+    with jax.named_scope("squares_dp_tensor"):
+        line, gain_states = ordered((line, gain_states))
+        got = to_all(line, n_dp * n_tensor, ("dp", "tensor"))
+        gain = jnp.sum(got[:, 0, 128:].reshape(n_dp, n_tensor, chunk), axis=1)
+        lane_squares = jnp.sum(got[:, :, :128], axis=0)
+        for h in range(chunk // 128):
+            half = gain[:, 128 * h : 128 * (h + 1)]
+            lane_squares += jnp.sum(half * half, axis=0, keepdims=True)
+        ones = jnp.ones((128, 128), jnp.float32)
+        total_squares = jnp.dot(lane_squares, ones, precision=lax.Precision.HIGHEST)
+    clip_limit = clip_level * math.sqrt(D * HEADS * HEAD + D)
+    clip_factor = clip_limit / (jnp.sqrt(total_squares) + 1e-06)
+    clip_row = jnp.concatenate([clip_factor] * halves, axis=1)
+    zero = jnp.float32(0)
+    with jax.named_scope("weights_fsdp"):
+        mine = adamw(*state, own, clip_row, 0.1, zero)[0].astype(jnp.bfloat16)
+        mine, gain = ordered((mine, gain))
+        got = to_all(mine, n_fsdp, "fsdp")
     with jax.named_scope("weights_dp"):
-        mine = got[:, :piece].reshape(n_fsdp * piece, cols)
-        terms = [t.astype(jnp.bfloat16) for t in (high, low)]
-        got = to_all(jnp.concatenate([mine, *terms], axis=0), n_dp, "dp")
+        mine = jnp.concatenate([got.reshape(n_fsdp * piece, cols), terms], axis=0)
+        mine, gain, gain_states, owner = ordered((mine, gain, gain_states, owner))
+        got = to_all(mine, n_dp, "dp")
         weights = got[:, : n_fsdp * piece].reshape(n_dp, n_fsdp, piece, cols)
         weights = weights.transpose(1, 0, 2, 3).reshape(rows, cols)
         high, low = (
@@ -106,7 +118,16 @@
             for i in range(2)
         )
         owned_rows = high.astype(jnp.float32) + low.astype(jnp.float32)
-    matrix_state = adamw(master, moment_one, moment_two, owned_rows, clip_factor, 0.1, teacher)
+    with jax.named_scope("gain"):
+        gain = gain.reshape(n_fsdp, block)
+        gain_states = [gain_states[:, i] for i in range(3)]
+        gain_weights = adamw(*gain_states, gain, clip_factor, 0.0, zero)[0]
+        gain_weights = gain_weights.astype(jnp.bfloat16).reshape(rows)
+        owned_gain = lax.dynamic_slice_in_dim(gain.reshape(rows), owner, block)
+        gain_state = adamw(
+            gain_master, gain_moment_one, gain_moment_two, owned_gain, clip_factor[0], 0.0, gain_teacher
+        )
+    matrix_state = adamw(master, moment_one, moment_two, owned_rows, clip_row, 0.1, teacher)
     return (
         weights,
         gain_weights,

time: 135 us -> 129 us (0.956)
  blocking collectives: 77.6 us -> 102 us
  waiting for transfers between devices: 31.9 us -> 14.9 us
  starting transfers between devices: 14.2 us -> 3.69 us
  local copies, waits for them, and re-layouts: 5.58 us -> 3.91 us
    all_to_all x3 -> x5, blocking collectives: 77.6 us -> 102 us  [exchange(): return lax.all_to_all(blocks, axis, 0, 0, tiled=True)]
    all_to_all x3 -> x1, waiting for transfers between devices: 31.9 us -> 14.9 us  [exchange(): return lax.all_to_all(blocks, axis, 0, 0, tiled=True)]
    all_to_all x3 -> x1, starting transfers between devices: 14.2 us -> 3.69 us  [exchange(): return lax.all_to_all(blocks, axis, 0, 0, tiled=True)]
  transfers between devices with their start and end apart: 3 -> 1, of which waited for: 3 -> 1; matrix products, arithmetic and copies ran while one was open for 0% -> 1% of each run, Pallas kernels for 0% -> 0%
where the time goes in v3:
time: 129 us
  blocking collectives  102 us (79%)
  waiting for transfers between devices  14.9 us (12%)
  local copies, waits for them, and re-layouts  3.91 us (3%)
  starting transfers between devices  3.69 us (3%)
  other arithmetic  2.7 us (2%)
    all_to_all x5, blocking collectives, exchange(): return lax.all_to_all(blocks, axis, 0, 0, tiled=True)  102 us
    all_to_all x1, waiting for transfers between devices, exchange(): return lax.all_to_all(blocks, axis, 0, 0, tiled=True)  14.9 us
    all_to_all x1, starting transfers between devices, exchange(): return lax.all_to_all(blocks, axis, 0, 0, tiled=True)  3.69 us
  transfers between devices with their start and end apart: 1, of which 1 were waited for; matrix products, arithmetic and copies ran while one was open for 1% of the time, Pallas kernels for 0%

profile of v3, /device:TPU:32, one launch (start us, length us, event | category | flops | bytes accessed | tf_op | source)
XLA Modules:
  0.0 128.7 jit_solution(15631011855597878324)
XLA Ops:
  0.6 0.0 copy-start.4
  0.7 1.3 %copy.32 = bf16[8,16,16,256]{3,2,1,0:T(8,128)(2,1)S(1)} copy(bf16[8,16,16,256]{3,2,0,1:T(8,128)(2,1)} %bitcast.54) | data formatting | bytes 2097152 | tf_op jit(solution)/shard_map/sum_dp/transpose | solution.py:64
  2.0 0.0 copy-done.4
  2.0 0.1 pad_maximum_fusion
  2.1 24.5 %all_to_all.30 = bf16[8,257,256]{2,1,0:T(8,128)(2,1)S(1)} all-to-all(bf16[8,257,256]{2,1,0:T(8,128)(2,1)S(1)} %pad_maximum_fusion), channel_id=1, replica_groups=mesh['dp'=8,'fsdp'=16,'tensor'=4] {'dp'}, dimensions={0} | all-to-all | bytes 2105344 | tf_op jit(solution)/shard_map/sum_dp/all_to_all | solution.py:35
  26.6 0.2 convert_reduce_fusion
  26.7 0.0 copy-start.5
  26.7 0.0 copy-start.6
  26.8 0.0 copy-start.7
  26.8 0.0 copy-start
  26.8 0.0 copy-start.1
  26.8 0.0 copy-start.2
  26.9 32.8 %all_to_all.31 = f32[16,32,128]{2,1,0:T(8,128)S(1)} all-to-all(f32[16,32,128]{2,1,0:T(8,128)S(1)} %pad_maximum_fusion.1), channel_id=1, replica_groups=mesh['dp'=8,'fsdp'=16,'tensor'=4] {'fsdp'}, dimensions={0} | all-to-all | bytes 524288 | tf_op jit(solution)/shard_map/sum_fsdp/all_to_all | solution.py:35
  59.7 0.0 copy-done.5
  59.8 0.0 copy-done.6
  59.8 0.0 copy-done.7
  59.8 0.0 copy-done
  59.9 0.0 copy-done.1
  59.9 0.0 copy-done.2
  59.9 16.3 %all_to_all.32 = f32[16,1,768]{2,1,0:T(1,128)S(1)} all-to-all(f32[16,1,768]{2,1,0:T(1,128)S(1)} %broadcast_in_dim.50), channel_id=1, replica_groups=mesh['dp'=8,'fsdp'=16,'tensor'=4] {'fsdp'}, dimensions={0} | all-to-all | bytes 98304 | tf_op jit(solution)/shard_map/squares_fsdp/all_to_all | solution.py:35
  76.2 0.1 slice_reduce_fusion.1
  76.4 11.0 %all_to_all.33 = f32[32,1,384]{2,1,0:T(1,128)S(1)} all-to-all(f32[32,1,384]{2,1,0:T(1,128)S(1)} %broadcast_in_dim.52), channel_id=1, replica_groups=mesh['dp'=8,'fsdp'=16,'tensor'=4] {'dp','tensor'}, dimensions={0} | all-to-all | bytes 98304 | tf_op jit(solution)/shard_map/squares_dp_tensor/all_to_all | solution.py:35
  87.4 0.1 slice_reduce_fusion
  87.6 0.1 fusion.2
  87.9 17.8 %all_to_all.34 = bf16[16,16,256]{2,1,0:T(8,128)(2,1)S(1)} all-to-all(bf16[16,16,256]{2,1,0:T(8,128)(2,1)S(1)} %broadcast_in_dim.54), channel_id=1, replica_groups=mesh['dp'=8,'fsdp'=16,'tensor'=4] {'fsdp'}, dimensions={0} | all-to-all | bytes 262144 | tf_op jit(solution)/shard_map/weights_fsdp/all_to_all | solution.py:35
  105.7 1.1 broadcast_in_dim.55
  106.7 0.0 copy-start.8
  106.7 3.7 %all-to-all-start.5 = ((bf16[8,288,256]{2,1,0:T(8,128)(2,1)}), bf16[8,288,256]{2,1,0:T(8,128)(2,1)S(1)}, u32[]{:S(2)}, u32[]{:S(2)}) async-start(bf16[8,288,256]{2,1,0:T(8,128)(2,1)} %broadcast_in_dim.55), calls=%async_computation.5 | async-start | bytes 2359296 | tf_op jit(solution)/shard_map/weights_dp/all_to_all | solution.py:35
  110.5 0.0 copy-done.8
  110.5 0.6 multiply_add_fusion.2
  111.1 0.6 fusion.24
  111.7 14.9 %all-to-all-done.5 = bf16[8,288,256]{2,1,0:T(8,128)(2,1)S(1)} async-done(((bf16[8,288,256]{2,1,0:T(8,128)(2,1)}), bf16[8,288,256]{2,1,0:T(8,128)(2,1)S(1)}, u32[]{:S(2)}, u32[]{:S(2)}) %all-to-all-start.5) | async-done | bytes 1179680 | tf_op jit(solution)/shard_map/weights_dp/all_to_all | solution.py:35
  126.7 0.1 slice.82
  126.7 0.0 copy-start.3
  126.8 1.1 copy.35
  127.9 0.0 copy-done.3
  127.9 0.9 multiply_add_fusion
  (33 shorter events, 0.5 us)
Async XLA Ops:
  0.6 1.4 %copy-start.4 = (bf16[1,1,1,2048]{3,2,1,0:T(2,128)(2,1)S(1)}, bf16[1,1,1,2048]{3,2,1,0:T(2,128)(2,1)}, u32[]{:S(2)}) copy-start(bf16[1,1,1,2048]{3,2,1,0:T(2,128)(2,1)} %param.11) | copy-start | bytes 12292
  26.7 33.0 %copy-start.5 = (f32[128]{0:T(128)S(1)}, f32[128]{0:T(128)}, u32[]{:S(2)}) copy-start(f32[128]{0:T(128)} %param.16) | copy-start | bytes 1540
  26.7 33.0 %copy-start.6 = (f32[128]{0:T(128)S(1)}, f32[128]{0:T(128)}, u32[]{:S(2)}) copy-start(f32[128]{0:T(128)} %param.17) | copy-start | bytes 1540
  26.8 33.0 %copy-start.7 = (f32[128]{0:T(128)S(1)}, f32[128]{0:T(128)}, u32[]{:S(2)}) copy-start(f32[128]{0:T(128)} %param.18) | copy-start | bytes 1540
  26.8 33.0 %copy-start = (f32[128,256]{1,0:T(8,128)S(1)}, f32[128,256]{1,0:T(8,128)}, u32[]{:S(2)}) copy-start(f32[128,256]{1,0:T(8,128)} %param.12) | copy-start | bytes 393220
  26.8 33.1 %copy-start.1 = (f32[128,256]{1,0:T(8,128)S(1)}, f32[128,256]{1,0:T(8,128)}, u32[]{:S(2)}) copy-start(f32[128,256]{1,0:T(8,128)} %param.14) | copy-start | bytes 393220
  26.8 33.1 %copy-start.2 = (f32[128,256]{1,0:T(8,128)S(1)}, f32[128,256]{1,0:T(8,128)}, u32[]{:S(2)}) copy-start(f32[128,256]{1,0:T(8,128)} %param.13) | copy-start | bytes 393220
  106.7 3.7 %copy-start.8 = (f32[128]{0:T(128)S(1)}, f32[128]{0:T(128)}, u32[]{:S(2)}) copy-start(f32[128]{0:T(128)} %param.19) | copy-start | bytes 1540
  106.7 19.9 %all-to-all-start.5 = ((bf16[8,288,256]{2,1,0:T(8,128)(2,1)}), bf16[8,288,256]{2,1,0:T(8,128)(2,1)S(1)}, u32[]{:S(2)}, u32[]{:S(2)}) async-start(bf16[8,288,256]{2,1,0:T(8,128)(2,1)} %broadcast_in_dim.55), calls=%async_computation.5 | async-start | bytes 2359296 | tf_op jit(solution)/shard_map/weights_dp/all_to_all | solution.py:35
  126.7 1.1 copy-start.3

commit v4 on v3

v4 whole, which is shorter than its diff:
```python
import math

import jax
import jax.numpy as jnp
from jax import lax
from jax.experimental import pallas as pl
from jax.experimental.pallas import tpu as pltpu
from jax.sharding import PartitionSpec as P

D = 2048
HEADS = 8
HEAD = 128
STEP = 20


beta_one = 0.9
beta_two = 0.95
learn_rate = 0.001
teacher_keep = 0.996
clip_level = 2.0
tiny_epsilon = 1e-08


def adamw(parameter, first_moment, second_moment, gradient, clip_factor, weight_decay, shadow):
    scaled = gradient * clip_factor
    first_new = beta_one * first_moment + (1.0 - beta_one) * scaled
    second_new = beta_two * second_moment + (1.0 - beta_two) * scaled * scaled
    corr_one = 1.0 - beta_one**STEP
    corr_two = 1.0 - beta_two**STEP
    direction = first_new / corr_one / (jnp.sqrt(second_new / corr_two) + tiny_epsilon)
    parameter_new = parameter - learn_rate * (direction + weight_decay * parameter)
    shadow_new = teacher_keep * shadow + (1.0 - teacher_keep) * parameter_new
    return (parameter_new, first_new, second_new, shadow_new)


def finish_kernel(*refs):
    got, clip = refs[:2]
    state, gain_weights, gain_state = refs[2:6], refs[6], refs[7]
    weights, gain_out, *outs = refs[8:18]
    terms, old, new, sems = refs[18], refs[19:23], refs[23:27], refs[27]
    n_dp, pieces, piece, cols = got.shape
    started = []

    def start(source, target):
        copy = pltpu.make_async_copy(source, target, sems.at[len(started)])
        copy.start()
        started.append(copy)

    start(got.at[:, pl.ds(pieces - 2, 2)], terms)
    for i in range(4):
        start(state[i], old[i])
    loads = len(started)
    for d in range(n_dp):
        start(got.at[d, pl.ds(0, pieces - 2)], weights.at[:, d])
    start(gain_weights, gain_out)
    for i in range(4):
        start(gain_state.at[pl.ds(i, 1)], outs[4 + i])
    for copy in started[:loads]:
        copy.wait()
    rows = terms[:, 0].astype(jnp.float32) + terms[:, 1].astype(jnp.float32)
    rows = rows.reshape(n_dp * piece, cols)
    values = adamw(*(ref[...] for ref in old[:3]), rows, clip[...], 0.1, old[3][...])
    for i in range(4):
        new[i][...] = values[i]
        start(new[i], outs[i])
    for copy in started[loads:]:
        copy.wait()


def finish(got, clip, state, gain_weights, gain_state):
    n_dp, pieces, piece, cols = got.shape
    owned = jax.ShapeDtypeStruct(state[0].shape, jnp.float32)
    gain = jax.ShapeDtypeStruct((1, gain_state.shape[1]), jnp.float32)
    anywhere = pl.BlockSpec(memory_space=pl.ANY)
    return pl.pallas_call(
        finish_kernel,
        out_shape=[
            jax.ShapeDtypeStruct((pieces - 2, n_dp, piece, cols), jnp.bfloat16),
            jax.ShapeDtypeStruct(gain_weights.shape, jnp.bfloat16),
            *[owned] * 4,
            *[gain] * 4,
        ],
        in_specs=[anywhere, pl.BlockSpec(memory_space=pltpu.VMEM)] + [anywhere] * 6,
        out_specs=[anywhere] * 10,
        scratch_shapes=[
            pltpu.VMEM((n_dp, 2, piece, cols), jnp.bfloat16),
            *[pltpu.VMEM(owned.shape, jnp.float32)] * 8,
            pltpu.SemaphoreType.DMA((14 + n_dp,)),
        ],
        compiler_params=pltpu.CompilerParams(vmem_limit_bytes=4 << 20),
        cost_estimate=pl.CostEstimate(flops=40 * 128 * 256, bytes_accessed=3 << 20, transcendentals=0),
    )(got, clip, *state, gain_weights, gain_state)


def exchange(blocks, axis):
    return lax.all_to_all(blocks, axis, 0, 0, tiled=True)


def to_all(block, count, axis):
    return exchange(jnp.broadcast_to(block[None], (count, *block.shape)), axis)


def shards(
    grad_part,
    gain_grad_part,
    master,
    moment_one,
    moment_two,
    teacher,
    gain_master,
    gain_moment_one,
    gain_moment_two,
    gain_teacher,
):
    n_dp, n_fsdp, n_tensor = (lax.axis_size(a) for a in ("dp", "fsdp", "tensor"))
    rows, cols = grad_part.shape[2:]
    block = rows // n_fsdp
    piece = block // n_dp
    lines = piece * cols // 128
    halves = cols // 128
    ordered = lax.optimization_barrier

    with jax.named_scope("sum_dp"):
        pieces = grad_part.reshape(n_fsdp, n_dp, piece, cols).transpose(1, 0, 2, 3)
        pieces = pieces.reshape(n_dp, n_fsdp * piece, cols)
        gain_rows = gain_grad_part.reshape(1, rows // cols, cols)
        gain_rows = jnp.broadcast_to(gain_rows, (n_dp, *gain_rows.shape[1:]))
        pieces = jnp.concatenate([pieces, gain_rows], axis=1)
        first, pieces = ordered((lax.axis_index("dp") * piece, pieces))
        got = exchange(pieces, "dp")
        summed = jnp.sum(got.astype(jnp.float32), axis=0)
    with jax.named_scope("sum_fsdp"):
        part = summed[: n_fsdp * piece].reshape(n_fsdp, piece, cols)
        part = jnp.concatenate([part[:, :, 128 * h : 128 * (h + 1)] for h in range(halves)], axis=1)
        gain_part = summed[n_fsdp * piece :].reshape(n_fsdp, 1, block)
        part = jnp.concatenate([part.reshape(n_fsdp, 1, lines * 128), gain_part], axis=2)
        summed = jnp.sum(exchange(part, "fsdp"), axis=0)
        summed, first = ordered((summed, first))
        own, own_gain = summed[:, : lines * 128].reshape(lines, 128), summed[:, lines * 128 :]
        state = [lax.dynamic_slice_in_dim(a, first, piece) for a in (master, moment_one, moment_two)]
        own_squares = jnp.sum(own * own, axis=0, keepdims=True)
        own = jnp.concatenate([own[piece * h : piece * (h + 1)] for h in range(halves)], axis=1)
        high = lax.reduce_precision(own, 8, 7)
        low = lax.reduce_precision(own - high, 8, 7)
        own = high + low
        terms = jnp.concatenate([high.astype(jnp.bfloat16), low.astype(jnp.bfloat16)], axis=0)
    with jax.named_scope("squares_dp_tensor"):
        line = jnp.concatenate([own_gain, own_squares], axis=1)
        line, own, terms, state = ordered((line, own, terms, state))
        got = to_all(line, n_dp * n_tensor, ("dp", "tensor"))
        owned_gain = jnp.sum(got[:n_tensor, :, :block], axis=0)
        squares = jnp.sum(got[:, :, block:], axis=0) + owned_gain * owned_gain
    with jax.named_scope("squares_fsdp"):
        line = [a[None] for a in (gain_master, gain_moment_one, gain_moment_two)]
        line = jnp.concatenate([squares, owned_gain, *line], axis=1)
        line, owned_gain = ordered((line, owned_gain))
        got = to_all(line, n_fsdp, "fsdp")
        lane_squares = jnp.sum(got[:, :, :block], axis=0)
        gain, *gain_states = [got[:, 0, block * i : block * (i + 1)] for i in range(1, 5)]
        ones = jnp.ones((128, 128), jnp.float32)
        total_squares = jnp.dot(lane_squares, ones, precision=lax.Precision.HIGHEST)
    clip_limit = clip_level * math.sqrt(D * HEADS * HEAD + D)
    clip_factor = clip_limit / (jnp.sqrt(total_squares) + 1e-06)
    clip_row = jnp.concatenate([clip_factor] * halves, axis=1)
    zero = jnp.float32(0)
    with jax.named_scope("gain"):
        gain_weights = adamw(*gain_states, gain, clip_factor, 0.0, zero)[0].astype(jnp.bfloat16)
        gain_state = (gain_master, gain_moment_one, gain_moment_two)
        gain_state = [a[None] for a in gain_state]
        gain_state = adamw(*gain_state, owned_gain, clip_factor, 0.0, gain_teacher[None])
        gain_state = jnp.concatenate(gain_state, axis=0)
    with jax.named_scope("weights_fsdp"):
        mine = adamw(*state, own, clip_row, 0.1, zero)[0].astype(jnp.bfloat16)
        mine, gain_weights, gain_state = ordered((mine, gain_weights, gain_state))
        got = to_all(mine, n_fsdp, "fsdp")
    with jax.named_scope("weights_dp"):
        mine = jnp.concatenate([got.reshape(n_fsdp * piece, cols), terms], axis=0)
        got = to_all(mine, n_dp, "dp")
        got = got.reshape(n_dp, n_fsdp + 2, piece, cols)
        state = (master, moment_one, moment_two, teacher)
        weights, gain_weights, *states = finish(got, clip_row, state, gain_weights, gain_state)
        matrix_state, gain_state = states[:4], [a.reshape(block) for a in states[4:]]
    return (
        weights.reshape(rows, cols),
        gain_weights.reshape(rows),
        *matrix_state,
        *gain_state,
    )


def solution(mesh):
    return jax.shard_map(
        shards,
        mesh=mesh,
        in_specs=(
            P("dp", "fsdp", None, "tensor"),
            P("dp", "fsdp", "tensor", None),
            P("fsdp", "tensor"),
            P("fsdp", "tensor"),
            P("fsdp", "tensor"),
            P("fsdp", "tensor"),
            P("fsdp"),
            P("fsdp"),
            P("fsdp"),
            P("fsdp"),
        ),
        out_specs=(
            P(None, "tensor"),
            P(),
            P("fsdp", "tensor"),
            P("fsdp", "tensor"),
            P("fsdp", "tensor"),
            P("fsdp", "tensor"),
            P("fsdp"),
            P("fsdp"),
            P("fsdp"),
            P("fsdp"),
        ),
        check_vma=False,
    )
```

time: 129 us -> 127 us (0.984)
  the two profiles are of different devices: /device:TPU:32 before, /device:TPU:2 now
where the time goes in v4:
time: 127 us
  blocking collectives  120 us (94%)
  Pallas kernels  2.03 us (2%)
  local copies, waits for them, and re-layouts  1.66 us (1%)
  other arithmetic  1.64 us (1%)
    all_to_all x6, blocking collectives, exchange(): return lax.all_to_all(blocks, axis, 0, 0, tiled=True)  120 us

profile of v4, /device:TPU:2, one launch (start us, length us, event | category | flops | bytes accessed | tf_op | source)
XLA Modules:
  0.0 126.7 jit_solution(3414760573056830171)
XLA Ops:
  0.6 0.7 reduce.4
  1.4 1.3 %copy.31 = bf16[8,16,16,256]{3,2,1,0:T(8,128)(2,1)S(1)} copy(bf16[8,16,16,256]{3,2,0,1:T(8,128)(2,1)} %bitcast.93) | data formatting | bytes 2097152 | tf_op jit(solution)/shard_map/sum_dp/transpose | solution.py:124
  2.7 0.1 pad_maximum_fusion
  2.8 23.7 %all_to_all.30 = bf16[8,264,256]{2,1,0:T(8,128)(2,1)S(1)} all-to-all(bf16[8,264,256]{2,1,0:T(8,128)(2,1)S(1)} %pad_maximum_fusion), channel_id=1, replica_groups=mesh['dp'=8,'fsdp'=16,'tensor'=4] {'dp'}, dimensions={0} | all-to-all | bytes 2162688 | tf_op jit(solution)/shard_map/sum_dp/all_to_all | solution.py:96
  26.5 0.1 convert_reduce_fusion
  26.7 0.0 copy-start
  26.7 0.0 copy-start.1
  26.7 0.0 copy-start.2
  26.8 0.0 copy-start.5
  26.8 0.0 copy-start.6
  26.8 0.0 copy-start.7
  26.8 0.0 copy-start.4
  26.8 0.3 pad_maximum_fusion.1
  27.1 32.4 %all_to_all.31 = f32[16,1,4224]{2,1,0:T(1,128)S(1)} all-to-all(f32[16,1,4224]{2,1,0:T(1,128)S(1)} %pad_maximum_fusion.1), channel_id=1, replica_groups=mesh['dp'=8,'fsdp'=16,'tensor'=4] {'fsdp'}, dimensions={0} | all-to-all | bytes 540672 | tf_op jit(solution)/shard_map/sum_fsdp/all_to_all | solution.py:96
  59.5 0.2 reduce_sum.61
  59.8 0.0 copy-done
  59.8 0.0 copy-done.1
  59.8 0.0 copy-done.2
  59.9 11.0 %all_to_all.32 = f32[32,1,256]{2,1,0:T(1,128)S(1)} all-to-all(f32[32,1,256]{2,1,0:T(1,128)S(1)} %broadcast_in_dim.58), channel_id=1, replica_groups=mesh['dp'=8,'fsdp'=16,'tensor'=4] {'dp','tensor'}, dimensions={0} | all-to-all | bytes 65536 | tf_op jit(solution)/shard_map/squares_dp_tensor/all_to_all | solution.py:96
  71.0 0.0 copy-done.5
  71.0 0.0 copy-done.6
  71.0 0.0 copy-done.7
  71.1 17.8 %all_to_all.33 = f32[16,1,640]{2,1,0:T(1,128)S(1)} all-to-all(f32[16,1,640]{2,1,0:T(1,128)S(1)} %broadcast_in_dim.63), channel_id=1, replica_groups=mesh['dp'=8,'fsdp'=16,'tensor'=4] {'fsdp'}, dimensions={0} | all-to-all | bytes 81920 | tf_op jit(solution)/shard_map/squares_fsdp/all_to_all | solution.py:96
  88.9 0.0 copy-done.4
  88.9 0.2 bitcast_add_fusion.1
  89.2 16.5 %all_to_all.34 = bf16[16,16,256]{2,1,0:T(8,128)(2,1)S(1)} all-to-all(bf16[16,16,256]{2,1,0:T(8,128)(2,1)S(1)} %broadcast_in_dim.65), channel_id=1, replica_groups=mesh['dp'=8,'fsdp'=16,'tensor'=4] {'fsdp'}, dimensions={0} | all-to-all | bytes 262144 | tf_op jit(solution)/shard_map/weights_fsdp/all_to_all | solution.py:96
  105.7 0.1 broadcast_in_dim.66
  105.8 0.0 copy-start.3
  105.8 18.8 %all_to_all.35 = bf16[8,288,256]{2,1,0:T(8,128)(2,1)S(1)} all-to-all(bf16[8,288,256]{2,1,0:T(8,128)(2,1)S(1)} %broadcast_in_dim.66), channel_id=1, replica_groups=mesh['dp'=8,'fsdp'=16,'tensor'=4] {'dp'}, dimensions={0} | all-to-all | bytes 2359296 | tf_op jit(solution)/shard_map/weights_dp/all_to_all | solution.py:96
  124.6 0.0 copy-done.3
  124.6 2.0 %weights_dp.1 = (bf16[16,8,16,256]{3,2,1,0:T(8,128)(2,1)}, bf16[16,128]{1,0:T(8,128)(2,1)}, f32[128,256]{1,0:T(8,128)}, f32[128,256]{1,0:T(8,128)}, f32[128,256]...) custom-call(bf16[8,18,16,256]{3,2,1,0:T(8,128)(2,1)S(1)} %bitcast.90, ...), custom_call_target="tpu_custom_call" | custom-call | flops 1310720 | bytes 3145728 | tf_op jit(solution)/shard_map/weights_dp/pallas_call | solution.py:75
  (35 shorter events, 0.5 us)
Async XLA Ops:
  26.7 33.1 %copy-start = (f32[128,256]{1,0:T(8,128)S(1)}, f32[128,256]{1,0:T(8,128)}, u32[]{:S(2)}) copy-start(f32[128,256]{1,0:T(8,128)} %refs_2_.1) | copy-start | bytes 393220
  26.7 33.1 %copy-start.1 = (f32[128,256]{1,0:T(8,128)S(1)}, f32[128,256]{1,0:T(8,128)}, u32[]{:S(2)}) copy-start(f32[128,256]{1,0:T(8,128)} %refs_4_.1) | copy-start | bytes 393220
  26.7 33.1 %copy-start.2 = (f32[128,256]{1,0:T(8,128)S(1)}, f32[128,256]{1,0:T(8,128)}, u32[]{:S(2)}) copy-start(f32[128,256]{1,0:T(8,128)} %refs_3_.1) | copy-start | bytes 393220
  26.8 44.2 %copy-start.5 = (f32[128]{0:T(128)S(1)}, f32[128]{0:T(128)}, u32[]{:S(2)}) copy-start(f32[128]{0:T(128)} %param.16) | copy-start | bytes 1540
  26.8 44.2 %copy-start.6 = (f32[128]{0:T(128)S(1)}, f32[128]{0:T(128)}, u32[]{:S(2)}) copy-start(f32[128]{0:T(128)} %param.17) | copy-start | bytes 1540
  26.8 44.3 %copy-start.7 = (f32[128]{0:T(128)S(1)}, f32[128]{0:T(128)}, u32[]{:S(2)}) copy-start(f32[128]{0:T(128)} %param.18) | copy-start | bytes 1540
  26.8 62.1 %copy-start.4 = (f32[128]{0:T(128)S(1)}, f32[128]{0:T(128)}, u32[]{:S(2)}) copy-start(f32[128]{0:T(128)} %param.19) | copy-start | bytes 1540
  105.8 18.8 %copy-start.3 = (f32[128,256]{1,0:T(8,128)S(1)}, f32[128,256]{1,0:T(8,128)}, u32[]{:S(2)}) copy-start(f32[128,256]{1,0:T(8,128)} %refs_5_.1) | copy-start | bytes 393220

commit v5 on v4

--- a/solution.py
+++ b/solution.py
@@ -37,33 +37,27 @@
     got, clip = refs[:2]
     state, gain_weights, gain_state = refs[2:6], refs[6], refs[7]
     weights, gain_out, *outs = refs[8:18]
-    terms, old, new, sems = refs[18], refs[19:23], refs[23:27], refs[27]
+    new, sems = refs[18:22], refs[22]
     n_dp, pieces, piece, cols = got.shape
-    started = []
+    copies = []
 
     def start(source, target):
-        copy = pltpu.make_async_copy(source, target, sems.at[len(started)])
+        copy = pltpu.make_async_copy(source, target, sems.at[len(copies)])
         copy.start()
-        started.append(copy)
-
-    start(got.at[:, pl.ds(pieces - 2, 2)], terms)
-    for i in range(4):
-        start(state[i], old[i])
-    loads = len(started)
+        copies.append(copy)
+
     for d in range(n_dp):
         start(got.at[d, pl.ds(0, pieces - 2)], weights.at[:, d])
+    rows = got[:, pieces - 2].astype(jnp.float32) + got[:, pieces - 1].astype(jnp.float32)
+    rows = rows.reshape(n_dp * piece, cols)
+    values = adamw(*(ref[...] for ref in state[:3]), rows, clip[...], 0.1, state[3][...])
+    for i in range(4):
+        new[i][...] = values[i]
+        start(new[i], outs[i])
     start(gain_weights, gain_out)
     for i in range(4):
         start(gain_state.at[pl.ds(i, 1)], outs[4 + i])
-    for copy in started[:loads]:
-        copy.wait()
-    rows = terms[:, 0].astype(jnp.float32) + terms[:, 1].astype(jnp.float32)
-    rows = rows.reshape(n_dp * piece, cols)
-    values = adamw(*(ref[...] for ref in old[:3]), rows, clip[...], 0.1, old[3][...])
-    for i in range(4):
-        new[i][...] = values[i]
-        start(new[i], outs[i])
-    for copy in started[loads:]:
+    for copy in copies:
         copy.wait()
 
 
@@ -80,14 +74,13 @@
             *[owned] * 4,
             *[gain] * 4,
         ],
-        in_specs=[anywhere, pl.BlockSpec(memory_space=pltpu.VMEM)] + [anywhere] * 6,
+        in_specs=[pl.BlockSpec(memory_space=pltpu.VMEM)] * 8,
         out_specs=[anywhere] * 10,
         scratch_shapes=[
-            pltpu.VMEM((n_dp, 2, piece, cols), jnp.bfloat16),
-            *[pltpu.VMEM(owned.shape, jnp.float32)] * 8,
-            pltpu.SemaphoreType.DMA((14 + n_dp,)),
+            *[pltpu.VMEM(owned.shape, jnp.float32)] * 4,
+            pltpu.SemaphoreType.DMA((9 + n_dp,)),
         ],
-        compiler_params=pltpu.CompilerParams(vmem_limit_bytes=4 << 20),
+        compiler_params=pltpu.CompilerParams(vmem_limit_bytes=8 << 20),
         cost_estimate=pl.CostEstimate(flops=40 * 128 * 256, bytes_accessed=3 << 20, transcendentals=0),
     )(got, clip, *state, gain_weights, gain_state)
 
@@ -123,6 +116,7 @@
     with jax.named_scope("sum_dp"):
         pieces = grad_part.reshape(n_fsdp, n_dp, piece, cols).transpose(1, 0, 2, 3)
         pieces = pieces.reshape(n_dp, n_fsdp * piece, cols)
+        pieces, gain_grad_part = ordered((pieces, gain_grad_part))
         gain_rows = gain_grad_part.reshape(1, rows // cols, cols)
         gain_rows = jnp.broadcast_to(gain_rows, (n_dp, *gain_rows.shape[1:]))
         pieces = jnp.concatenate([pieces, gain_rows], axis=1)

time: 127 us -> 126 us (level)
  no operation moved by 1% of the time
where the time goes in v5:
time: 126 us; the launch traced here: 125 us
  blocking collectives  120 us (95%)
  local copies, waits for them, and re-layouts  1.66 us (1%)
  Pallas kernels  1.29 us (1%)
    all_to_all x6, blocking collectives, exchange(): return lax.all_to_all(blocks, axis, 0, 0, tiled=True)  120 us

profile of v5, /device:TPU:2, one launch (start us, length us, event | category | flops | bytes accessed | tf_op | source)
XLA Modules:
  0.0 125.2 jit_solution(5779864185882932005)
XLA Ops:
  0.6 0.0 copy-start.4
  0.7 1.3 %copy.31 = bf16[8,16,16,256]{3,2,1,0:T(8,128)(2,1)S(1)} copy(bf16[8,16,16,256]{3,2,0,1:T(8,128)(2,1)} %bitcast.93) | data formatting | bytes 2097152 | tf_op jit(solution)/shard_map/sum_dp/transpose | solution.py:117
  2.0 0.0 copy-done.4
  2.1 0.1 pad_maximum_fusion
  2.1 23.7 %all_to_all.30 = bf16[8,264,256]{2,1,0:T(8,128)(2,1)S(1)} all-to-all(bf16[8,264,256]{2,1,0:T(8,128)(2,1)S(1)} %pad_maximum_fusion), channel_id=1, replica_groups=mesh['dp'=8,'fsdp'=16,'tensor'=4] {'dp'}, dimensions={0} | all-to-all | bytes 2162688 | tf_op jit(solution)/shard_map/sum_dp/all_to_all | solution.py:89
  25.8 0.1 convert_reduce_fusion
  26.0 0.0 copy-start
  26.1 0.0 copy-start.1
  26.1 0.0 copy-start.2
  26.1 0.0 copy-start.6
  26.1 0.0 copy-start.7
  26.1 0.0 copy-start.8
  26.1 0.0 copy-start.5
  26.2 0.3 pad_maximum_fusion.1
  26.4 32.4 %all_to_all.31 = f32[16,1,4224]{2,1,0:T(1,128)S(1)} all-to-all(f32[16,1,4224]{2,1,0:T(1,128)S(1)} %pad_maximum_fusion.1), channel_id=1, replica_groups=mesh['dp'=8,'fsdp'=16,'tensor'=4] {'fsdp'}, dimensions={0} | all-to-all | bytes 540672 | tf_op jit(solution)/shard_map/sum_fsdp/all_to_all | solution.py:89
  58.8 0.2 reduce_sum.61
  59.1 0.0 copy-done
  59.2 0.0 copy-done.1
  59.2 0.0 copy-done.2
  59.2 11.0 %all_to_all.32 = f32[32,1,256]{2,1,0:T(1,128)S(1)} all-to-all(f32[32,1,256]{2,1,0:T(1,128)S(1)} %broadcast_in_dim.58), channel_id=1, replica_groups=mesh['dp'=8,'fsdp'=16,'tensor'=4] {'dp','tensor'}, dimensions={0} | all-to-all | bytes 65536 | tf_op jit(solution)/shard_map/squares_dp_tensor/all_to_all | solution.py:89
  70.3 0.0 copy-done.6
  70.3 0.0 copy-done.7
  70.4 0.0 copy-done.8
  70.4 17.8 %all_to_all.33 = f32[16,1,640]{2,1,0:T(1,128)S(1)} all-to-all(f32[16,1,640]{2,1,0:T(1,128)S(1)} %broadcast_in_dim.63), channel_id=1, replica_groups=mesh['dp'=8,'fsdp'=16,'tensor'=4] {'fsdp'}, dimensions={0} | all-to-all | bytes 81920 | tf_op jit(solution)/shard_map/squares_fsdp/all_to_all | solution.py:89
  88.3 0.0 copy-done.5
  88.3 0.2 bitcast_add_fusion.1
  88.6 16.5 %all_to_all.34 = bf16[16,16,256]{2,1,0:T(8,128)(2,1)S(1)} all-to-all(bf16[16,16,256]{2,1,0:T(8,128)(2,1)S(1)} %broadcast_in_dim.65), channel_id=1, replica_groups=mesh['dp'=8,'fsdp'=16,'tensor'=4] {'fsdp'}, dimensions={0} | all-to-all | bytes 262144 | tf_op jit(solution)/shard_map/weights_fsdp/all_to_all | solution.py:89
  105.0 0.1 broadcast_in_dim.66
  105.1 0.0 copy-start.3
  105.1 18.8 %all_to_all.35 = bf16[8,288,256]{2,1,0:T(8,128)(2,1)S(1)} all-to-all(bf16[8,288,256]{2,1,0:T(8,128)(2,1)S(1)} %broadcast_in_dim.66), channel_id=1, replica_groups=mesh['dp'=8,'fsdp'=16,'tensor'=4] {'dp'}, dimensions={0} | all-to-all | bytes 2359296 | tf_op jit(solution)/shard_map/weights_dp/all_to_all | solution.py:89
  124.0 0.0 copy-done.3
  124.0 1.3 %weights_dp.1 = (bf16[16,8,16,256]{3,2,1,0:T(8,128)(2,1)}, bf16[16,128]{1,0:T(8,128)(2,1)}, f32[128,256]{1,0:T(8,128)}, f32[128,256]{1,0:T(8,128)}, f32[128,256]...) custom-call(bf16[8,18,16,256]{3,2,1,0:T(8,128)(2,1)S(1)} %bitcast.90, ...), custom_call_target="tpu_custom_call" | custom-call | flops 1310720 | bytes 3145728 | tf_op jit(solution)/shard_map/weights_dp/pallas_call | solution.py:69
  (36 shorter events, 0.5 us)
Async XLA Ops:
  0.6 1.3 %copy-start.4 = (bf16[1,1,1,2048]{3,2,1,0:T(2,128)(2,1)S(1)}, bf16[1,1,1,2048]{3,2,1,0:T(2,128)(2,1)}, u32[]{:S(2)}) copy-start(bf16[1,1,1,2048]{3,2,1,0:T(2,128)(2,1)} %param.11) | copy-start | bytes 12292
  26.0 33.1 %copy-start = (f32[128,256]{1,0:T(8,128)S(1)}, f32[128,256]{1,0:T(8,128)}, u32[]{:S(2)}) copy-start(f32[128,256]{1,0:T(8,128)} %refs_2_.1) | copy-start | bytes 393220
  26.1 33.1 %copy-start.1 = (f32[128,256]{1,0:T(8,128)S(1)}, f32[128,256]{1,0:T(8,128)}, u32[]{:S(2)}) copy-start(f32[128,256]{1,0:T(8,128)} %refs_4_.1) | copy-start | bytes 393220
  26.1 33.1 %copy-start.2 = (f32[128,256]{1,0:T(8,128)S(1)}, f32[128,256]{1,0:T(8,128)}, u32[]{:S(2)}) copy-start(f32[128,256]{1,0:T(8,128)} %refs_3_.1) | copy-start | bytes 393220
  26.1 44.2 %copy-start.6 = (f32[128]{0:T(128)S(1)}, f32[128]{0:T(128)}, u32[]{:S(2)}) copy-start(f32[128]{0:T(128)} %param.16) | copy-start | bytes 1540
  26.1 44.2 %copy-start.7 = (f32[128]{0:T(128)S(1)}, f32[128]{0:T(128)}, u32[]{:S(2)}) copy-start(f32[128]{0:T(128)} %param.17) | copy-start | bytes 1540
  26.1 44.3 %copy-start.8 = (f32[128]{0:T(128)S(1)}, f32[128]{0:T(128)}, u32[]{:S(2)}) copy-start(f32[128]{0:T(128)} %param.18) | copy-start | bytes 1540
  26.1 62.1 %copy-start.5 = (f32[128]{0:T(128)S(1)}, f32[128]{0:T(128)}, u32[]{:S(2)}) copy-start(f32[128]{0:T(128)} %param.19) | copy-start | bytes 1540
  105.1 18.8 %copy-start.3 = (f32[128,256]{1,0:T(8,128)S(1)}, f32[128,256]{1,0:T(8,128)}, u32[]{:S(2)}) copy-start(f32[128,256]{1,0:T(8,128)} %refs_5_.1) | copy-start | bytes 393220

commit v6 on v5

--- a/solution.py
+++ b/solution.py
@@ -117,16 +117,13 @@
         pieces = grad_part.reshape(n_fsdp, n_dp, piece, cols).transpose(1, 0, 2, 3)
         pieces = pieces.reshape(n_dp, n_fsdp * piece, cols)
         pieces, gain_grad_part = ordered((pieces, gain_grad_part))
-        gain_rows = gain_grad_part.reshape(1, rows // cols, cols)
-        gain_rows = jnp.broadcast_to(gain_rows, (n_dp, *gain_rows.shape[1:]))
-        pieces = jnp.concatenate([pieces, gain_rows], axis=1)
-        first, pieces = ordered((lax.axis_index("dp") * piece, pieces))
+        gain_part = gain_grad_part.reshape(n_fsdp, 1, block).astype(jnp.float32)
+        first, pieces, gain_part = ordered((lax.axis_index("dp") * piece, pieces, gain_part))
         got = exchange(pieces, "dp")
         summed = jnp.sum(got.astype(jnp.float32), axis=0)
     with jax.named_scope("sum_fsdp"):
-        part = summed[: n_fsdp * piece].reshape(n_fsdp, piece, cols)
+        part = summed.reshape(n_fsdp, piece, cols)
         part = jnp.concatenate([part[:, :, 128 * h : 128 * (h + 1)] for h in range(halves)], axis=1)
-        gain_part = summed[n_fsdp * piece :].reshape(n_fsdp, 1, block)
         part = jnp.concatenate([part.reshape(n_fsdp, 1, lines * 128), gain_part], axis=2)
         summed = jnp.sum(exchange(part, "fsdp"), axis=0)
         summed, first = ordered((summed, first))
@@ -142,8 +139,9 @@
         line = jnp.concatenate([own_gain, own_squares], axis=1)
         line, own, terms, state = ordered((line, own, terms, state))
         got = to_all(line, n_dp * n_tensor, ("dp", "tensor"))
-        owned_gain = jnp.sum(got[:n_tensor, :, :block], axis=0)
-        squares = jnp.sum(got[:, :, block:], axis=0) + owned_gain * owned_gain
+        got = jnp.sum(got, axis=0)
+        owned_gain = got[:, :block]
+        squares = got[:, block:] + owned_gain * owned_gain
     with jax.named_scope("squares_fsdp"):
         line = [a[None] for a in (gain_master, gain_moment_one, gain_moment_two)]
         line = jnp.concatenate([squares, owned_gain, *line], axis=1)

time: 126 us -> 125 us (level)
  no operation moved by 1% of the time
where the time goes in v6:
time: 125 us; the launch traced here: 124 us
  blocking collectives  119 us (95%)
  local copies, waits for them, and re-layouts  1.59 us (1%)
  Pallas kernels  1.29 us (1%)
    all_to_all x6, blocking collectives, exchange(): return lax.all_to_all(blocks, axis, 0, 0, tiled=True)  119 us

profile of v6, /device:TPU:2, one launch (start us, length us, event | category | flops | bytes accessed | tf_op | source)
XLA Modules:
  0.0 124.3 jit_solution(6884877386444747245)
XLA Ops:
  0.6 0.0 copy-start.4
  0.7 1.3 %copy.31 = bf16[8,16,16,256]{3,2,1,0:T(8,128)(2,1)S(1)} copy(bf16[8,16,16,256]{3,2,0,1:T(8,128)(2,1)} %bitcast.89) | data formatting | bytes 2097152 | tf_op jit(solution)/shard_map/sum_dp/transpose | solution.py:117
  2.0 0.0 copy-done.4
  2.0 23.1 %all_to_all.30 = bf16[8,256,256]{2,1,0:T(8,128)(2,1)S(1)} all-to-all(bf16[8,256,256]{2,1,0:T(8,128)(2,1)S(1)} %bitcast.87), channel_id=1, replica_groups=mesh['dp'=8,'fsdp'=16,'tensor'=4] {'dp'}, dimensions={0} | all-to-all | bytes 2097152 | tf_op jit(solution)/shard_map/sum_dp/all_to_all | solution.py:89
  25.1 0.1 convert_reduce_fusion
  25.2 0.0 copy-start
  25.3 0.0 copy-start.1
  25.3 0.0 copy-start.2
  25.3 0.0 copy-start.6
  25.3 0.0 copy-start.7
  25.3 0.0 copy-start.8
  25.3 0.0 copy-start.5
  25.4 0.3 pad_maximum_fusion
  25.6 32.4 %all_to_all.31 = f32[16,1,4224]{2,1,0:T(1,128)S(1)} all-to-all(f32[16,1,4224]{2,1,0:T(1,128)S(1)} %pad_maximum_fusion), channel_id=1, replica_groups=mesh['dp'=8,'fsdp'=16,'tensor'=4] {'fsdp'}, dimensions={0} | all-to-all | bytes 540672 | tf_op jit(solution)/shard_map/sum_fsdp/all_to_all | solution.py:89
  58.0 0.2 reduce_sum.50
  58.2 0.0 copy-done
  58.3 0.0 copy-done.1
  58.3 0.0 copy-done.2
  58.4 10.9 %all_to_all.32 = f32[32,1,256]{2,1,0:T(1,128)S(1)} all-to-all(f32[32,1,256]{2,1,0:T(1,128)S(1)} %broadcast_in_dim.24), channel_id=1, replica_groups=mesh['dp'=8,'fsdp'=16,'tensor'=4] {'dp','tensor'}, dimensions={0} | all-to-all | bytes 65536 | tf_op jit(solution)/shard_map/squares_dp_tensor/all_to_all | solution.py:89
  69.3 0.1 reduce_sum.53
  69.3 0.0 copy-done.6
  69.4 0.0 copy-done.7
  69.4 0.0 copy-done.8
  69.4 17.9 %all_to_all.33 = f32[16,1,640]{2,1,0:T(1,128)S(1)} all-to-all(f32[16,1,640]{2,1,0:T(1,128)S(1)} %broadcast_in_dim.54), channel_id=1, replica_groups=mesh['dp'=8,'fsdp'=16,'tensor'=4] {'fsdp'}, dimensions={0} | all-to-all | bytes 81920 | tf_op jit(solution)/shard_map/squares_fsdp/all_to_all | solution.py:89
  87.4 0.0 copy-done.5
  87.4 0.2 bitcast_add_fusion.1
  87.7 16.5 %all_to_all.34 = bf16[16,16,256]{2,1,0:T(8,128)(2,1)S(1)} all-to-all(bf16[16,16,256]{2,1,0:T(8,128)(2,1)S(1)} %broadcast_in_dim.56), channel_id=1, replica_groups=mesh['dp'=8,'fsdp'=16,'tensor'=4] {'fsdp'}, dimensions={0} | all-to-all | bytes 262144 | tf_op jit(solution)/shard_map/weights_fsdp/all_to_all | solution.py:89
  104.1 0.1 broadcast_in_dim.57
  104.2 0.0 copy-start.3
  104.2 18.8 %all_to_all.35 = bf16[8,288,256]{2,1,0:T(8,128)(2,1)S(1)} all-to-all(bf16[8,288,256]{2,1,0:T(8,128)(2,1)S(1)} %broadcast_in_dim.57), channel_id=1, replica_groups=mesh['dp'=8,'fsdp'=16,'tensor'=4] {'dp'}, dimensions={0} | all-to-all | bytes 2359296 | tf_op jit(solution)/shard_map/weights_dp/all_to_all | solution.py:89
  123.1 0.0 copy-done.3
  123.1 1.3 %weights_dp.1 = (bf16[16,8,16,256]{3,2,1,0:T(8,128)(2,1)}, bf16[16,128]{1,0:T(8,128)(2,1)}, f32[128,256]{1,0:T(8,128)}, f32[128,256]{1,0:T(8,128)}, f32[128,256]...) custom-call(bf16[8,18,16,256]{3,2,1,0:T(8,128)(2,1)S(1)} %bitcast.85, ...), custom_call_target="tpu_custom_call" | custom-call | flops 1310720 | bytes 3145728 | tf_op jit(solution)/shard_map/weights_dp/pallas_call | solution.py:69
  (27 shorter events, 0.4 us)
Async XLA Ops:
  0.6 1.3 %copy-start.4 = (bf16[1,1,1,2048]{3,2,1,0:T(2,128)(2,1)S(1)}, bf16[1,1,1,2048]{3,2,1,0:T(2,128)(2,1)}, u32[]{:S(2)}) copy-start(bf16[1,1,1,2048]{3,2,1,0:T(2,128)(2,1)} %param.11) | copy-start | bytes 12292
  25.2 33.0 %copy-start = (f32[128,256]{1,0:T(8,128)S(1)}, f32[128,256]{1,0:T(8,128)}, u32[]{:S(2)}) copy-start(f32[128,256]{1,0:T(8,128)} %refs_2_.1) | copy-start | bytes 393220
  25.3 33.0 %copy-start.1 = (f32[128,256]{1,0:T(8,128)S(1)}, f32[128,256]{1,0:T(8,128)}, u32[]{:S(2)}) copy-start(f32[128,256]{1,0:T(8,128)} %refs_4_.1) | copy-start | bytes 393220
  25.3 33.0 %copy-start.2 = (f32[128,256]{1,0:T(8,128)S(1)}, f32[128,256]{1,0:T(8,128)}, u32[]{:S(2)}) copy-start(f32[128,256]{1,0:T(8,128)} %refs_3_.1) | copy-start | bytes 393220
  25.3 44.0 %copy-start.6 = (f32[128]{0:T(128)S(1)}, f32[128]{0:T(128)}, u32[]{:S(2)}) copy-start(f32[128]{0:T(128)} %param.16) | copy-start | bytes 1540
  25.3 44.1 %copy-start.7 = (f32[128]{0:T(128)S(1)}, f32[128]{0:T(128)}, u32[]{:S(2)}) copy-start(f32[128]{0:T(128)} %param.17) | copy-start | bytes 1540
  25.3 44.1 %copy-start.8 = (f32[128]{0:T(128)S(1)}, f32[128]{0:T(128)}, u32[]{:S(2)}) copy-start(f32[128]{0:T(128)} %param.18) | copy-start | bytes 1540
  25.3 62.0 %copy-start.5 = (f32[128]{0:T(128)S(1)}, f32[128]{0:T(128)}, u32[]{:S(2)}) copy-start(f32[128]{0:T(128)} %param.19) | copy-start | bytes 1540
  104.2 18.8 %copy-start.3 = (f32[128,256]{1,0:T(8,128)S(1)}, f32[128,256]{1,0:T(8,128)}, u32[]{:S(2)}) copy-start(f32[128,256]{1,0:T(8,128)} %refs_5_.1) | copy-start | bytes 393220
